TPU v7x, 1024 devices: a whole 4x4x32 slice. The times are simulated.
1024 devices in a mesh: section: 16 (over z_lo), dp: 16 (over x, y), head: 4 (over z_hi, core).
Axes of the slice: x: 4, y: 4, z: 32 (z_hi: 2, z_lo: 16; z = z_hi * 16 + z_lo), core: 2. Of those that a mesh axis runs over, the one named last changes fastest.
Arguments:
- segments: int32 [17, 2048], P(None, 'dp'), may hold values from 0 to 63, never falling along the last dimension, each value on 1 to 64 neighbouring positions
- section_input_stream: bfloat16 [16, 2048, 2048], P('section', 'dp', 'head'), may hold values from -16 to 16
- entering: bfloat16 [2048, 2048], P('dp'), may hold values from -16 to 16
- pending_first_values: bfloat16 [16, 2048, 512], P('section', 'dp', 'head'), may hold values from -6 to 6
- norm_gain_vector: float32 [16, 2048], P('section'), may hold values from 0.1 to 1.9
- query_weight: bfloat16 [16, 2048, 2048], P('section', None, 'head'), may hold values from -0.110485435 to 0.110485435
- key_weight: bfloat16 [16, 2048, 512], P('section', None, 'head'), may hold values from -0.110485435 to 0.110485435
- value_weight: bfloat16 [16, 2048, 512], P('section', None, 'head'), may hold values from -0.125 to 0.125
- output_weight: bfloat16 [16, 2048, 2048], P('section', None, 'head'), may hold values from -0.125 to 0.125
- query_key_scale: float32 [16, 16], P('section', 'head'), may hold values from 0.7 to 24
- value_blend_weight: float32 [16, 4], P('section', 'head'), may hold values from 0.3 to 1.5
- value_cotangent_rows: bfloat16 [16, 2, 2048, 512], P('section', None, 'dp', 'head'), may hold values from -0.125 to 0.125
Outputs:
- first_round: bfloat16 [16, 2048, 2048], P('section', 'dp', 'head')
- second_round: bfloat16 [16, 2048, 2048], P('section', 'dp', 'head')
- value_weight_grads: float32 [16, 2048, 512], P('section', 'dp', 'head')
Inputs may be any that keep to these rules, and one draw needn't show every extreme that they name: `segments`: along each row document ids never fall, and a document holds at most half of 128 tokens.
All inputs are finite; a program needn't handle non-finite values.
Results may differ from a plain program's by a relative error of at most 0.018.
Values may be sent and summed in bfloat16 or wider, within the bound.
No kernel may reach another device: no remote copies, remote signals or barrier semaphores. Data moves between devices by JAX's collectives and lax.ppermute only.
A program may use at most 32 MiB of HBM per device.

v0:
```python
import math

import jax
import jax.numpy as jnp
from jax import lax
from jax.sharding import PartitionSpec as P

D = 2048
HEAD_WIDTH = 128


epsilon = 1e-06


def passed_along(shard, axis, by):
    peers = lax.axis_size(axis)
    pairs = [(i, i + by) for i in range(peers) if 0 <= i + by < peers]
    return lax.ppermute(shard, axis, pairs)


def rms_rows(values):
    return values * lax.rsqrt(jnp.mean(values * values, axis=-1, keepdims=True) + epsilon)


def attend(
    full_rows,
    segment_row,
    feature_gain,
    query_proj,
    key_proj,
    value_proj,
    scales,
    mixing,
    earlier_values,
    is_first,
):
    tokens = full_rows.shape[0]
    local_heads = query_proj.shape[1] // HEAD_WIDTH
    local_kv = key_proj.shape[1] // HEAD_WIDTH
    group_size = local_heads // local_kv
    normed = (rms_rows(full_rows.astype(jnp.float32)) * feature_gain).astype(jnp.bfloat16)
    queries = jnp.dot(normed, query_proj, preferred_element_type=jnp.float32).reshape(
        tokens, local_kv, group_size, HEAD_WIDTH
    )
    key_rows = jnp.dot(normed, key_proj, preferred_element_type=jnp.float32).reshape(
        tokens, local_kv, HEAD_WIDTH
    )
    values = jnp.dot(normed, value_proj, preferred_element_type=jnp.float32)
    queries = rms_rows(queries)
    key_rows = rms_rows(key_rows)
    own_values = values.astype(jnp.bfloat16)
    blended = (
        values + jnp.repeat(mixing, HEAD_WIDTH)[None, :] * earlier_values.astype(jnp.float32)
    ).astype(jnp.bfloat16)
    mixed_values = jnp.where(is_first, own_values, blended)
    carried = jnp.where(is_first, own_values, earlier_values)
    factor = (scales / math.sqrt(HEAD_WIDTH)).reshape(local_kv, group_size)
    scores = jnp.einsum("qkgd,tkd->kgqt", queries, key_rows) * factor[:, :, None, None]
    positions = jnp.arange(tokens)
    allowed = (positions[:, None] >= positions[None, :]) & (
        segment_row[:, None] == segment_row[None, :]
    )
    scores = jnp.where(allowed, scores, -jnp.inf)
    row_max = jnp.max(scores, axis=-1, keepdims=True)
    exponent = jnp.exp(scores - row_max)
    weights = (exponent / jnp.sum(exponent, axis=-1, keepdims=True)).astype(jnp.bfloat16)
    attended = jnp.einsum(
        "kgqt,tkd->qkgd",
        weights,
        mixed_values.reshape(tokens, local_kv, HEAD_WIDTH),
        preferred_element_type=jnp.float32,
    )
    attended = attended.astype(jnp.bfloat16).reshape(tokens, local_heads * HEAD_WIDTH)
    return (attended, normed, carried)


def collect(piece):
    return lax.all_gather(piece, "head", axis=1, tiled=True)


def grad_term(normed_rows, cotangent):

    def partial_term(first_row, row_count):
        return jnp.einsum("td,tc->dc", normed_rows, cotangent, preferred_element_type=jnp.float32)

    return partial_term


def per_device(
    segments,
    section_input_stream,
    entering,
    pending_first_values,
    norm_gain_vector,
    query_weight,
    key_weight,
    value_weight,
    output_weight,
    query_key_scale,
    value_blend_weight,
    value_cotangent_rows,
):
    section_index = lax.axis_index("section")
    head_index = lax.axis_index("head")
    is_first = section_index == 0
    shard_width = output_weight.shape[2]
    total_batches = segments.shape[0]
    grad_rows = D // lax.axis_size("dp")
    feature_gain = norm_gain_vector[0]
    query_proj = query_weight[0]
    key_proj = key_weight[0]
    value_proj = value_weight[0]
    out_proj = output_weight[0]
    scales = query_key_scale[0]
    mixing = value_blend_weight[0]

    def project(own_rows, attended):
        all_heads = collect(attended)
        return (
            own_rows.astype(jnp.float32)
            + jnp.dot(all_heads, out_proj, preferred_element_type=jnp.float32)
        ).astype(jnp.bfloat16)

    first_segments = lax.dynamic_index_in_dim(segments, section_index, 0, keepdims=False)
    own_first = section_input_stream[0]
    gathered_first = collect(own_first)
    attended_first, normed_first, carried_first = attend(
        gathered_first,
        first_segments,
        feature_gain,
        query_proj,
        key_proj,
        value_proj,
        scales,
        mixing,
        pending_first_values[0],
        is_first,
    )
    output_first = project(own_first, attended_first)
    whole_first = collect(output_first)
    received_whole, received_values = passed_along((whole_first, carried_first), "section", 1)
    gathered_second = jnp.where(is_first, entering, received_whole)
    own_second = lax.dynamic_slice_in_dim(gathered_second, head_index * shard_width, shard_width, 1)
    second_index = (section_index + total_batches - 1) % total_batches
    second_segments = lax.dynamic_index_in_dim(segments, second_index, 0, keepdims=False)
    attended_second, normed_second, carried_second = attend(
        gathered_second,
        second_segments,
        feature_gain,
        query_proj,
        key_proj,
        value_proj,
        scales,
        mixing,
        received_values,
        is_first,
    )
    output_second = project(own_second, attended_second)
    first_term = grad_term(normed_first, value_cotangent_rows[0, 0])
    second_term = grad_term(normed_second, value_cotangent_rows[0, 1])
    first_row = jnp.int32(0)
    gradients = lax.psum_scatter(
        first_term(first_row, grad_rows * lax.axis_size("dp"))
        + second_term(first_row, grad_rows * lax.axis_size("dp")),
        "dp",
        scatter_dimension=0,
        tiled=True,
    )
    return (output_first[None], output_second[None], gradients[None])


def solution(mesh):
    return jax.shard_map(
        per_device,
        mesh=mesh,
        in_specs=(
            P(None, "dp"),
            P("section", "dp", "head"),
            P("dp", None),
            P("section", "dp", "head"),
            P("section", None),
            P("section", None, "head"),
            P("section", None, "head"),
            P("section", None, "head"),
            P("section", None, "head"),
            P("section", "head"),
            P("section", "head"),
            P("section", None, "dp", "head"),
        ),
        out_specs=(
            P("section", "dp", "head"),
            P("section", "dp", "head"),
            P("section", "dp", "head"),
        ),
        check_vma=False,
    )
```

profile of v0, /device:TPU:6, one launch (start us, length us, event | category | flops | bytes accessed | tf_op | source)
XLA Modules:
  0.0 265.7 jit_solution(13060140364008875240)
XLA Ops:
  7.2 0.0 copy-start
  7.2 0.0 reduce-scatter.2.cloned.1.call-start
  7.2 0.8 fusion.76
  8.1 0.1 fusion.50
  8.2 33.7 %all-gather = bf16[1,128,2048]{2,1,0:T(8,128)(2,1)S(1)} all-gather(bf16[1,128,512]{2,1,0:T(8,128)(2,1)} %param.13), channel_id=2, replica_groups=mesh['section'=16,'dp'=16,'head'=4] {'head'}, dimensions={2}, use_global_device_ids=true | all-gather | bytes 655360 | tf_op jit(solution)/shard_map/all_gather | solution.py:78
  41.8 0.2 fusion.23
  42.0 0.0 copy-done
  42.1 0.0 copy-start.9
  42.1 1.2 fusion.86
  43.3 0.0 copy-start.8
  43.3 0.1 mul.164
  43.4 0.2 reduce_sum.74
  43.6 0.0 copy-start.7
  43.7 1.5 multiply_reduce_fusion.1
  45.2 0.0 copy-done.9
  45.9 0.2 mul.165
  46.1 0.0 copy-start.1
  46.1 0.0 copy-start.2
  46.1 0.2 fusion.87
  46.3 0.1 fusion.40
  46.4 0.4 bitcast_select_fusion
  46.8 0.2 convolution_convert_fusion.1
  47.0 0.0 copy-start.6
  47.0 26.1 %all_gather.13 = bf16[128,2048]{0,1:T(8,128)(2,1)S(1)} all-gather(bf16[128,512]{0,1:T(8,128)(2,1)S(1)} %bitcast.185), channel_id=1, replica_groups=mesh['section'=16,'dp'=16,'head'=4] {'head'}, dimensions={1}, use_global_device_ids=true | all-gather | bytes 655360 | tf_op jit(solution)/shard_map/all_gather | solution.py:78
  73.1 0.0 copy-done.2
  73.1 0.5 fusion.17
  73.6 0.0 copy-start.3
  73.6 41.4 %all_gather.14 = bf16[128,2048]{1,0:T(8,128)(2,1)S(1)} all-gather(bf16[128,512]{1,0:T(8,128)(2,1)S(1)} %fusion.17), channel_id=1, replica_groups=mesh['section'=16,'dp'=16,'head'=4] {'head'}, dimensions={1}, use_global_device_ids=true | all-gather | bytes 655360 | tf_op jit(solution)/shard_map/all_gather | solution.py:78
  115.1 21.2 %collective-permute-start = (bf16[128,2048]{1,0:T(8,128)(2,1)S(1)}, bf16[128,2048]{1,0:T(8,128)(2,1)S(1)}, u32[]{:S(2)}, u32[]{:S(2)}) collective-permute-start(bf16[128,2048]{1,0:T(8,128)(2,1)S(1)} %all_gather.14), channel_id=1, source_target_pairs={{0,64},{64,128},{128,192},{192,256},{256,320},{320,384},{384,448},... | collective-permute-start | bytes 1572872 | tf_op jit(solution)/shard_map/ppermute | solution.py:18
  136.3 1.9 collective-permute-start.1
  138.2 0.4 fusion.58
  138.6 9.7 %collective-permute-done = bf16[128,2048]{1,0:T(8,128)(2,1)S(1)} collective-permute-done((bf16[128,2048]{1,0:T(8,128)(2,1)S(1)}, bf16[128,2048]{1,0:T(8,128)(2,1)S(1)}, u32[]{:S(2)}, u32[]{:S(2)}) %collective-permute-start) | collective-permute-done | bytes 524320 | tf_op jit(solution)/shard_map/ppermute | solution.py:18
  148.3 0.3 fusion.20
  148.6 1.4 convolution_add_fusion
  150.0 0.0 reduce-scatter.2.cloned.1.call-update
  150.0 0.1 fusion.49
  150.1 0.5 fusion.88
  150.6 0.1 mul.182
  150.7 0.2 reduce_sum.78
  150.9 1.5 multiply_reduce_fusion
  152.4 0.2 mul.183
  152.6 0.2 fusion.89
  152.9 0.1 fusion.41
  152.9 0.0 collective-permute-done.1
  152.9 1.6 convolution_convert_fusion
  154.6 32.7 %all_gather.15 = bf16[128,2048]{0,1:T(8,128)(2,1)S(1)} all-gather(bf16[128,512]{0,1:T(8,128)(2,1)S(1)} %bitcast.184), channel_id=1, replica_groups=mesh['section'=16,'dp'=16,'head'=4] {'head'}, dimensions={1}, use_global_device_ids=true | all-gather | bytes 655360 | tf_op jit(solution)/shard_map/all_gather | solution.py:78
  187.3 2.7 %fusion.42 = bf16[1,128,512]{2,1,0:T(8,128)(2,1)} fusion(bf16[128,2048]{1,0:T(8,128)(2,1)S(1)} %get-tuple-element.4, s32[]{:T(128)S(6)} %select_n.54, bf16[128,2048]{0,1:T(8,128)(2,1)S(1)} %all_gather.15, bf16[1,2048,512]{2,1,0:T(8,128)(2,1)} %param.20), kind=kOutput, calls=%fused_computation.55 | convolution fusion | flops 268632064 | bytes 2883588 | tf_op jit(solution)/shard_map/dot_general | solution.py:121
  190.0 68.8 %reduce-scatter.2.cloned.1.call-done = f32[128,128]{1,0:T(8,128)} async-done(((f32[2048,128]{1,0:T(8,128)}), f32[128,128]{1,0:T(8,128)}) %reduce-scatter.2.cloned.1.call-update) | async-done | bytes 65552 | tf_op jit(solution)/shard_map/reduce_scatter | solution.py:162
  (16 shorter events, 0.1 us)
Async XLA Ops:
  7.2 34.9 %copy-start = (bf16[1,2048,512]{2,1,0:T(8,128)(2,1)S(1)}, bf16[1,2048,512]{2,1,0:T(8,128)(2,1)}, u32[]{:S(2)}) copy-start(bf16[1,2048,512]{2,1,0:T(8,128)(2,1)} %param.17) | copy-start | bytes 6291460
  7.2 251.7 %reduce-scatter.2.cloned.1.call-start = ((), (), s32[]{:S(2)}) async-start(), calls=%async_computation.1 | async-start | bytes 1114112 | tf_op jit(solution)/shard_map/reduce_scatter | solution.py:162
  42.0 1.6 copy-start.5
  42.1 3.1 %copy-start.9 = (f32[1,4]{1,0:T(1,128)S(1)}, f32[1,4]{1,0:T(1,128)}, u32[]{:S(2)}) copy-start(f32[1,4]{1,0:T(1,128)} %param.21) | copy-start | bytes 52
  43.3 3.1 %copy-start.8 = (bf16[1,128,128]{2,1,0:T(8,128)(2,1)S(1)}, bf16[1,128,128]{2,1,0:T(8,128)(2,1)}, u32[]{:S(2)}) copy-start(bf16[1,128,128]{2,1,0:T(8,128)(2,1)} %param.15) | copy-start | bytes 98308
  43.6 2.8 %copy-start.7 = (bf16[1,2048,128]{2,1,0:T(8,128)(2,1)S(1)}, bf16[1,2048,128]{2,1,0:T(8,128)(2,1)}, u32[]{:S(2)}) copy-start(bf16[1,2048,128]{2,1,0:T(8,128)(2,1)} %param.19) | copy-start | bytes 1572868
  46.1 27.1 %copy-start.1 = (bf16[1,2048,512]{2,1,0:T(8,128)(2,1)S(1)}, bf16[1,2048,512]{2,1,0:T(8,128)(2,1)}, u32[]{:S(2)}) copy-start(bf16[1,2048,512]{2,1,0:T(8,128)(2,1)} %param.20) | copy-start | bytes 6291460
  46.1 27.1 %copy-start.2 = (bf16[1,128,512]{2,1,0:T(8,128)(2,1)S(1)}, bf16[1,128,512]{2,1,0:T(8,128)(2,1)}, u32[]{:S(2)}) copy-start(bf16[1,128,512]{2,1,0:T(8,128)(2,1)} %param.13) | copy-start | bytes 393220
  47.0 91.2 %copy-start.6 = (bf16[1,2,128,128]{3,2,1,0:T(8,128)(2,1)S(1)}, bf16[1,2,128,128]{3,2,1,0:T(8,128)(2,1)}, u32[]{:S(2)}) copy-start(bf16[1,2,128,128]{3,2,1,0:T(8,128)(2,1)} %param.23) | copy-start | bytes 196612
  73.1 75.2 %copy-start.4 = (bf16[128,2048]{1,0:T(8,128)(2,1)S(1)}, bf16[128,2048]{1,0:T(8,128)(2,1)}, u32[]{:S(2)}) copy-start(bf16[128,2048]{1,0:T(8,128)(2,1)} %param.14) | copy-start | bytes 1572868
  73.6 76.4 %copy-start.3 = (bf16[128,512]{1,0:T(8,128)(2,1)}, bf16[128,512]{1,0:T(8,128)(2,1)S(1)}, u32[]{:S(2)}) copy-start(bf16[128,512]{1,0:T(8,128)(2,1)S(1)} %fusion.17) | copy-start | bytes 393220
  115.1 33.2 %collective-permute-start = (bf16[128,2048]{1,0:T(8,128)(2,1)S(1)}, bf16[128,2048]{1,0:T(8,128)(2,1)S(1)}, u32[]{:S(2)}, u32[]{:S(2)}) collective-permute-start(bf16[128,2048]{1,0:T(8,128)(2,1)S(1)} %all_gather.14), channel_id=1, source_target_pairs={{0,64},{64,128},{128,192},{192,256},{256,320},{320,384},{384,448},... | collective-permute-start | bytes 1572872 | tf_op jit(solution)/shard_map/ppermute | solution.py:18
  136.3 16.6 %collective-permute-start.1 = (bf16[128,128]{1,0:T(8,128)(2,1)S(1)}, bf16[128,128]{1,0:T(8,128)(2,1)S(1)}, u32[]{:S(2)}, u32[]{:S(2)}) collective-permute-start(bf16[128,128]{1,0:T(8,128)(2,1)S(1)} %get-tuple-element.19), channel_id=1, source_target_pairs={{0,64},{64,128},{128,192},{192,256},{256,320},{320,384},{384,448},... | collective-permute-start | bytes 98312 | tf_op jit(solution)/shard_map/ppermute | solution.py:18
Sparse Core Ops, SparseCore 0:
  150.2 108.6 reduce-scatter.1
where the time goes:
time: 266 us
  blocking collectives  134 us (50%)
  waiting for transfers between devices  78.5 us (30%)
  starting transfers between devices  23.1 us (9%)
  between operations  15 us (6%)
  matrix products  12.3 us (5%)
    all_gather x4, blocking collectives, collect(): return lax.all_gather(piece, 'head', axis=1, tiled=True)  134 us
    reduce_scatter x1, waiting for transfers between devices, per_device(): lax.psum_scatter(first_term(first_row, grad_rows * lax.axis_size('dp')) +...  68.8 us
    ppermute x2, starting transfers between devices, passed_along(): return lax.ppermute(shard, axis, pairs)  23.1 us
    ppermute x2, waiting for transfers between devices, passed_along(): return lax.ppermute(shard, axis, pairs)  9.68 us
  transfers between devices with their start and end apart: 3, of which 2 were waited for; matrix products, arithmetic and copies ran while one was open for 3% of the time, Pallas kernels for 0%

commit v1 on v0

--- a/solution.py
+++ b/solution.py
@@ -79,11 +79,7 @@
 
 
 def grad_term(normed_rows, cotangent):
-
-    def partial_term(first_row, row_count):
-        return jnp.einsum("td,tc->dc", normed_rows, cotangent, preferred_element_type=jnp.float32)
-
-    return partial_term
+    return jnp.einsum("td,tc->dc", normed_rows, cotangent, preferred_element_type=jnp.float32)
 
 
 def per_device(
@@ -137,10 +133,10 @@
         is_first,
     )
     output_first = project(own_first, attended_first)
-    whole_first = collect(output_first)
-    received_whole, received_values = passed_along((whole_first, carried_first), "section", 1)
-    gathered_second = jnp.where(is_first, entering, received_whole)
-    own_second = lax.dynamic_slice_in_dim(gathered_second, head_index * shard_width, shard_width, 1)
+    received_own, received_values = passed_along((output_first, carried_first), "section", 1)
+    entering_own = lax.dynamic_slice_in_dim(entering, head_index * shard_width, shard_width, 1)
+    own_second = jnp.where(is_first, entering_own, received_own)
+    gathered_second = collect(own_second)
     second_index = (section_index + total_batches - 1) % total_batches
     second_segments = lax.dynamic_index_in_dim(segments, second_index, 0, keepdims=False)
     attended_second, normed_second, carried_second = attend(
@@ -158,14 +154,11 @@
     output_second = project(own_second, attended_second)
     first_term = grad_term(normed_first, value_cotangent_rows[0, 0])
     second_term = grad_term(normed_second, value_cotangent_rows[0, 1])
-    first_row = jnp.int32(0)
-    gradients = lax.psum_scatter(
-        first_term(first_row, grad_rows * lax.axis_size("dp"))
-        + second_term(first_row, grad_rows * lax.axis_size("dp")),
-        "dp",
-        scatter_dimension=0,
-        tiled=True,
-    )
+    partial = first_term + second_term
+    replicas = lax.axis_size("dp")
+    pieces = partial.astype(jnp.bfloat16).reshape(replicas, grad_rows, partial.shape[1])
+    exchanged = lax.all_to_all(pieces, "dp", 0, 0, tiled=True)
+    gradients = jnp.sum(exchanged.astype(jnp.float32), axis=0)
     return (output_first[None], output_second[None], gradients[None])
 
 

time: 266 us -> 193 us (0.73)
  the two profiles are of different devices: /device:TPU:6 before, /device:TPU:931 now
where the time goes in v1:
time: 193 us
  blocking collectives  117 us (61%)
  starting transfers between devices  33.6 us (17%)
  matrix products  18.4 us (10%)
  waiting for transfers between devices  15.7 us (8%)
  other arithmetic  4.68 us (2%)
    all_gather x4, blocking collectives, collect(): return lax.all_gather(piece, 'head', axis=1, tiled=True)  117 us
    ppermute x2, starting transfers between devices, passed_along(): return lax.ppermute(shard, axis, pairs)  26.7 us
    ppermute x2, waiting for transfers between devices, passed_along(): return lax.ppermute(shard, axis, pairs)  15.7 us
    all_to_all x1, starting transfers between devices, per_device(): exchanged = lax.all_to_all(pieces, 'dp', 0, 0, tiled=True)  6.92 us
    dot_general x2, matrix products, grad_term(): jnp.einsum('td,tc->dc', normed_rows, cotangent, preferred_element_type=jn...  3.87 us
  transfers between devices with their start and end apart: 3, of which 1 were waited for; matrix products, arithmetic and copies ran while one was open for 8% of the time, Pallas kernels for 0%

profile of v1, /device:TPU:931, one launch (start us, length us, event | category | flops | bytes accessed | tf_op | source)
XLA Modules:
  0.0 192.7 jit_solution(13514509753120884145)
XLA Ops:
  0.6 0.0 copy-start
  0.6 0.0 copy-start.3
  0.7 0.8 multiply_bitcast_fusion
  1.5 34.3 %all-gather = bf16[1,128,2048]{2,1,0:T(8,128)(2,1)S(1)} all-gather(bf16[1,128,512]{2,1,0:T(8,128)(2,1)} %param.13), channel_id=2, replica_groups=mesh['section'=16,'dp'=16,'head'=4] {'head'}, dimensions={2}, use_global_device_ids=true | all-gather | bytes 655360 | tf_op jit(solution)/shard_map/all_gather | solution.py:78
  35.8 0.2 fusion.24
  36.0 1.5 multiply_reduce_fusion.1
  37.5 0.8 fusion.77
  38.2 0.1 fusion.51
  38.3 0.0 copy-done
  38.3 0.0 copy-start.7
  38.4 0.5 fusion.87
  38.9 0.1 mul.164
  39.0 0.2 reduce_sum.83
  39.8 0.2 mul.165
  40.0 0.0 copy-start.1
  40.1 0.0 copy-start.2
  40.1 0.2 fusion.88
  40.3 0.1 fusion.41
  40.4 2.2 %bitcast_select_fusion = (bf16[128,128]{1,0:T(8,128)(2,1)}, f32[128,128]{1,0:T(8,128)S(1)}) fusion(bf16[1,128,128]{2,1,0:T(8,128)(2,1)S(1)} %copy-done.7, pred[]{:T(512)S(6)} %eq.35, bf16[1,2048,128]{2,1,0:T(8,128)(2,1)} %param.19, bf16[1,128,2048]{2,1,0:T(8,128)(2,1)S(1)} %all-gather, f32[2048]{0:T(1024)S(1)} %bitcast.178, f32[128]{0:T(128)S(1)} %add_rsqrt_fusion.5), kind=kOutput, calls=%fused_computation.80 | convolution fusion | flops 68190208 | bytes 1188353 | tf_op jit(solution)/shard_map/dot_general | solution.py:48
  42.6 0.2 convolution_convert_fusion.1
  42.8 25.9 %all_gather.13 = bf16[128,2048]{0,1:T(8,128)(2,1)S(1)} all-gather(bf16[128,512]{0,1:T(8,128)(2,1)S(1)} %bitcast.186), channel_id=1, replica_groups=mesh['section'=16,'dp'=16,'head'=4] {'head'}, dimensions={1}, use_global_device_ids=true | all-gather | bytes 655360 | tf_op jit(solution)/shard_map/all_gather | solution.py:78
  68.7 0.0 copy-done.2
  68.7 0.5 fusion.18
  69.1 0.0 copy-start.4
  69.1 24.8 %collective-permute-start = (bf16[128,512]{1,0:T(8,128)(2,1)S(1)}, bf16[128,512]{1,0:T(8,128)(2,1)S(1)}, u32[]{:S(2)}, u32[]{:S(2)}) collective-permute-start(bf16[128,512]{1,0:T(8,128)(2,1)S(1)} %fusion.18), channel_id=1, source_target_pairs={{0,64},{64,128},{128,192},{192,256},{256,320},{320,384},{384,448},... | collective-permute-start | bytes 393224 | tf_op jit(solution)/shard_map/ppermute | solution.py:18
  94.0 1.9 collective-permute-start.1
  95.9 1.4 fusion.59
  97.3 0.7 fusion.50
  98.0 15.7 %collective-permute-done = bf16[128,512]{1,0:T(8,128)(2,1)S(1)} collective-permute-done((bf16[128,512]{1,0:T(8,128)(2,1)S(1)}, bf16[128,512]{1,0:T(8,128)(2,1)S(1)}, u32[]{:S(2)}, u32[]{:S(2)}) %collective-permute-start) | collective-permute-done | bytes 131104 | tf_op jit(solution)/shard_map/ppermute | solution.py:18
  113.7 1.0 dynamic-slice_select_fusion
  114.6 28.7 %all_gather.14 = bf16[128,2048]{1,0:T(8,128)(2,1)S(1)} all-gather(bf16[128,512]{1,0:T(8,128)(2,1)S(1)} %dynamic-slice_select_fusion), channel_id=1, replica_groups=mesh['section'=16,'dp'=16,'head'=4] {'head'}, dimensions={1}, use_global_device_ids=true | all-gather | bytes 655360 | tf_op jit(solution)/shard_map/all_gather | solution.py:78
  143.3 0.2 fusion.21
  143.5 2.1 %multiply_reduce_fusion = (f32[128]{0:T(128)S(1)}, f32[128,128]{0,1:T(8,128)}) fusion(bf16[1,2048,128]{2,1,0:T(8,128)(2,1)} %param.18, bf16[128,2048]{1,0:T(8,128)(2,1)S(1)} %all_gather.14, f32[128]{0:T(128)S(1)} %add_rsqrt_fusion.3, f32[2048]{0:T(1024)S(1)} %bitcast.180), kind=kOutput, calls=%fused_computation.65 | convolution fusion | flops 68190080 | bytes 1123328 | tf_op jit(solution)/shard_map/dot_general | solution.py:45
  145.6 1.2 fusion.89
  146.8 0.5 add_rsqrt_fusion.2
  147.3 0.1 mul.182
  147.4 0.2 reduce_sum.87
  147.6 2.5 %fusion = bf16[2048,128]{1,0:T(8,128)(2,1)} fusion(f32[2048,128]{1,0:T(8,128)} %fusion.59, bf16[1,2,128,128]{3,2,1,0:T(8,128)(2,1)S(1)} %copy-done.5, bf16[128,2048]{1,0:T(8,128)(2,1)S(1)} %all_gather.14, f32[128]{0:T(128)S(1)} %add_rsqrt_fusion.3, f32[2048]{0:T(1024)S(1)} %bitcast.182), kind=kOutput, calls=%fused_computation.1 | convolution fusion | flops 68681728 | bytes 2138624 | tf_op jit(solution)/shard_map/td,tc->dc/dot_general | solution.py:82
  150.1 6.9 %all-to-all-start = ((bf16[16,128,128]{2,1,0:T(8,128)(2,1)}), bf16[16,128,128]{2,1,0:T(8,128)(2,1)S(1)}, u32[]{:S(2)}, u32[]{:S(2)}) async-start(bf16[16,128,128]{2,1,0:T(8,128)(2,1)} %bitcast.33), calls=%async_computation | async-start | bytes 1048576 | tf_op jit(solution)/shard_map/all_to_all | solution.py:160
  157.0 0.2 mul.183
  157.2 1.2 fusion.90
  158.4 0.1 fusion.42
  158.5 0.0 collective-permute-done.1
  158.5 2.3 %convolution_convert_fusion = bf16[128,4,128]{2,0,1:T(8,128)(2,1)} fusion(f32[1,4,128,128]{2,3,1,0:T(8,128)S(1)} %get-tuple-element.16, f32[4,128]{1,0:T(4,128)S(1)} %fusion.42, f32[4,128]{1,0:T(4,128)S(1)} %get-tuple-element.15, bf16[128,128]{1,0:T(8,128)(2,1)} %collective-permute-done.1, bf16[1,2048,128]{2,1,0:T(8,128)(2,1)} %param.19, f32[]{:T(128)} %bitcast.173, ...), kind=kOutput, calls=%fused_computation.24 | convolution fusion | flops 85295104 | bytes 1487365 | tf_op jit(solution)/shard_map/kgqt,tkd->qkgd/dot_general | solution.py:67
  160.8 28.4 %all_gather.15 = bf16[128,2048]{0,1:T(8,128)(2,1)S(1)} all-gather(bf16[128,512]{0,1:T(8,128)(2,1)} %bitcast.185), channel_id=1, replica_groups=mesh['section'=16,'dp'=16,'head'=4] {'head'}, dimensions={1}, use_global_device_ids=true | all-gather | bytes 655360 | tf_op jit(solution)/shard_map/all_gather | solution.py:78
  189.2 2.7 %fusion.43 = bf16[1,128,512]{2,1,0:T(8,128)(2,1)} fusion(bf16[128,512]{1,0:T(8,128)(2,1)S(1)} %dynamic-slice_select_fusion, bf16[128,2048]{0,1:T(8,128)(2,1)S(1)} %all_gather.15, bf16[1,2048,512]{2,1,0:T(8,128)(2,1)} %param.20), kind=kOutput, calls=%fused_computation.56 | convolution fusion | flops 268632064 | bytes 2883584 | tf_op jit(solution)/shard_map/dot_general | solution.py:117
  191.9 0.0 all-to-all-done
  191.9 0.7 convert_reduce_fusion
  (13 shorter events, 0.1 us)
Async XLA Ops:
  0.6 37.7 %copy-start = (bf16[1,2048,512]{2,1,0:T(8,128)(2,1)S(1)}, bf16[1,2048,512]{2,1,0:T(8,128)(2,1)}, u32[]{:S(2)}) copy-start(bf16[1,2048,512]{2,1,0:T(8,128)(2,1)} %param.17) | copy-start | bytes 6291460
  0.6 37.7 %copy-start.3 = (f32[1,2048]{1,0:T(1,128)S(1)}, f32[1,2048]{1,0:T(1,128)}, u32[]{:S(2)}) copy-start(f32[1,2048]{1,0:T(1,128)} %param.16) | copy-start | bytes 24580
  38.3 2.0 %copy-start.7 = (bf16[1,128,128]{2,1,0:T(8,128)(2,1)S(1)}, bf16[1,128,128]{2,1,0:T(8,128)(2,1)}, u32[]{:S(2)}) copy-start(bf16[1,128,128]{2,1,0:T(8,128)(2,1)} %param.15) | copy-start | bytes 98308
  40.0 28.6 %copy-start.1 = (bf16[1,2048,512]{2,1,0:T(8,128)(2,1)S(1)}, bf16[1,2048,512]{2,1,0:T(8,128)(2,1)}, u32[]{:S(2)}) copy-start(bf16[1,2048,512]{2,1,0:T(8,128)(2,1)} %param.20) | copy-start | bytes 6291460
  40.1 28.6 %copy-start.2 = (bf16[1,128,512]{2,1,0:T(8,128)(2,1)S(1)}, bf16[1,128,512]{2,1,0:T(8,128)(2,1)}, u32[]{:S(2)}) copy-start(bf16[1,128,512]{2,1,0:T(8,128)(2,1)} %param.13) | copy-start | bytes 393220
  42.6 53.3 %copy-start.5 = (bf16[1,2,128,128]{3,2,1,0:T(8,128)(2,1)S(1)}, bf16[1,2,128,128]{3,2,1,0:T(8,128)(2,1)}, u32[]{:S(2)}) copy-start(bf16[1,2,128,128]{3,2,1,0:T(8,128)(2,1)} %param.23) | copy-start | bytes 196612
  69.1 74.4 %copy-start.4 = (bf16[128,512]{1,0:T(8,128)(2,1)}, bf16[128,512]{1,0:T(8,128)(2,1)S(1)}, u32[]{:S(2)}) copy-start(bf16[128,512]{1,0:T(8,128)(2,1)S(1)} %fusion.18) | copy-start | bytes 393220
  69.1 44.5 %collective-permute-start = (bf16[128,512]{1,0:T(8,128)(2,1)S(1)}, bf16[128,512]{1,0:T(8,128)(2,1)S(1)}, u32[]{:S(2)}, u32[]{:S(2)}) collective-permute-start(bf16[128,512]{1,0:T(8,128)(2,1)S(1)} %fusion.18), channel_id=1, source_target_pairs={{0,64},{64,128},{128,192},{192,256},{256,320},{320,384},{384,448},... | collective-permute-start | bytes 393224 | tf_op jit(solution)/shard_map/ppermute | solution.py:18
  94.0 64.5 %collective-permute-start.1 = (bf16[128,128]{1,0:T(8,128)(2,1)}, bf16[128,128]{1,0:T(8,128)(2,1)}, u32[]{:S(2)}, u32[]{:S(2)}) collective-permute-start(bf16[128,128]{1,0:T(8,128)(2,1)} %get-tuple-element.17), channel_id=1, source_target_pairs={{0,64},{64,128},{128,192},{192,256},{256,320},{320,384},{384,448},... | collective-permute-start | bytes 98312 | tf_op jit(solution)/shard_map/ppermute | solution.py:18
  143.5 4.1 %copy-start.6 = (f32[128]{0:T(128)}, f32[128]{0:T(128)S(1)}, u32[]{:S(2)}) copy-start(f32[128]{0:T(128)S(1)} %add_rsqrt_fusion.3) | copy-start | bytes 1540
  150.1 41.9 %all-to-all-start = ((bf16[16,128,128]{2,1,0:T(8,128)(2,1)}), bf16[16,128,128]{2,1,0:T(8,128)(2,1)S(1)}, u32[]{:S(2)}, u32[]{:S(2)}) async-start(bf16[16,128,128]{2,1,0:T(8,128)(2,1)} %bitcast.33), calls=%async_computation | async-start | bytes 1048576 | tf_op jit(solution)/shard_map/all_to_all | solution.py:160

commit v2 on v1

v2 whole, which is shorter than its diff:
```python
import math

import jax
import jax.numpy as jnp
from jax import lax
from jax.experimental import pallas as pl
from jax.experimental.pallas import tpu as pltpu
from jax.sharding import PartitionSpec as P

HEAD_WIDTH = 128
EPSILON = 1e-06
LANES = 128

VMEM = pl.BlockSpec(memory_space=pltpu.VMEM)
SMEM = pl.BlockSpec(memory_space=pltpu.SMEM)
HBM = pl.BlockSpec(memory_space=pltpu.HBM)


def collect(piece):
    return lax.all_gather(piece, "head", axis=1, tiled=True)


def collect_chip(piece):
    peers = lax.axis_size("head")
    chips = [[i, i + 1] for i in range(0, peers, 2)]
    return lax.all_gather(piece, "head", axis_index_groups=chips)


def collect_planes(piece):
    peers = lax.axis_size("head")
    pairs = [[i, i + peers // 2] for i in range(peers // 2)]
    return lax.all_gather(piece, "head", axis_index_groups=pairs)


def next_section(piece):
    peers = lax.axis_size("section")
    return lax.ppermute(piece, "section", [(i, i + 1) for i in range(peers - 1)])


def rms_rows(values):
    return values * lax.rsqrt(jnp.mean(values * values, axis=-1, keepdims=True) + EPSILON)


def begin(pairs, semaphores):
    copies = [pltpu.make_async_copy(src, dst, semaphores.at[i]) for i, (src, dst) in enumerate(pairs)]
    for copy in copies:
        copy.start()
    return copies


def root_mean_square(x_ref):
    tokens, width = x_ref.shape
    squares = jnp.zeros((tokens, LANES), jnp.float32)
    for start in range(0, width, LANES):
        part = x_ref[:, start : start + LANES].astype(jnp.float32)
        squares += part * part
    return lax.rsqrt(jnp.sum(squares, axis=-1, keepdims=True) / width + EPSILON)


def normalise(x_ref, root, gain_ref, normed_ref):
    for start in range(0, x_ref.shape[1], LANES):
        columns = slice(start, start + LANES)
        part = x_ref[:, columns].astype(jnp.float32)
        normed_ref[:, columns] = (part * root * gain_ref[:, columns]).astype(jnp.bfloat16)


def attend(
    normed_ref, row, is_first, key_ref, value_ref, query_ref, scale_ref, blend_ref, earlier_ref, waits, attended_ref,
    carried_ref,
):
    key_wait, value_wait, earlier_wait, query_wait = waits
    tokens = normed_ref.shape[0]
    local_heads = query_ref.shape[1] // HEAD_WIDTH
    across = jnp.broadcast_to(row, (tokens, tokens))
    down = across.T
    later = lax.broadcasted_iota(jnp.int32, (tokens, tokens), 0)
    sooner = lax.broadcasted_iota(jnp.int32, (tokens, tokens), 1)
    allowed = (later >= sooner) & (across == down)
    normed = normed_ref[...]
    key_wait()
    keys = rms_rows(jnp.dot(normed, key_ref[...], preferred_element_type=jnp.float32))
    value_wait()
    values = jnp.dot(normed, value_ref[...], preferred_element_type=jnp.float32)
    earlier_wait()
    own = values.astype(jnp.bfloat16)
    earlier = earlier_ref[...]
    blended = (values + blend_ref[0, 0] * earlier.astype(jnp.float32)).astype(jnp.bfloat16)
    mixed = jnp.where(is_first, own, blended)
    if carried_ref is not None:
        carried_ref[...] = jnp.where(is_first, own, earlier)
    query_wait()
    queries = jnp.dot(normed, query_ref[...], preferred_element_type=jnp.float32)
    for head in range(local_heads):
        columns = slice(head * HEAD_WIDTH, (head + 1) * HEAD_WIDTH)
        query = rms_rows(queries[:, columns])
        scores = lax.dot_general(
            query,
            keys,
            (((1,), (1,)), ((), ())),
            precision=lax.Precision.HIGHEST,
            preferred_element_type=jnp.float32,
        )
        scores = scores * (scale_ref[0, head] / math.sqrt(HEAD_WIDTH))
        scores = jnp.where(allowed, scores, -jnp.inf)
        exponent = jnp.exp(scores - jnp.max(scores, axis=-1, keepdims=True))
        weights = (exponent / jnp.sum(exponent, axis=-1, keepdims=True)).astype(jnp.bfloat16)
        attended_ref[:, columns] = jnp.dot(
            weights, mixed, preferred_element_type=jnp.float32
        ).astype(jnp.bfloat16)


def first_kernel(
    where_ref, scale_ref, blend_ref, x_ref, segments_in, gain_in, earlier_in, key_in, value_in, query_in,
    attended_ref, carried_ref, normed_out,
    segments_ref, gain_ref, earlier_ref, key_ref, value_ref, query_ref, normed_ref, semaphores,
):
    gain, segments, key, value, earlier, query = begin(
        [
            (gain_in, gain_ref),
            (segments_in, segments_ref),
            (key_in, key_ref),
            (value_in, value_ref),
            (earlier_in, earlier_ref),
            (query_in, query_ref),
        ],
        semaphores,
    )
    root = root_mean_square(x_ref)
    gain.wait()
    normalise(x_ref, root, gain_ref, normed_ref)
    normed_copy = pltpu.make_async_copy(normed_ref, normed_out, semaphores.at[6])
    normed_copy.start()
    segments.wait()
    row = segments_ref[pl.ds(where_ref[0], 1), :]
    attend(
        normed_ref, row, where_ref[0] == 0, key_ref, value_ref, query_ref, scale_ref, blend_ref, earlier_ref,
        (key.wait, value.wait, earlier.wait, query.wait), attended_ref, carried_ref,
    )
    normed_copy.wait()


def second_kernel(
    where_ref, scale_ref, blend_ref, received_ref, entering_ref, segments_ref, gain_ref, earlier_ref, key_ref,
    value_ref, query_ref,
    attended_ref, own_ref, normed_ref,
    x_ref,
):
    is_first = where_ref[0] == 0
    shard = own_ref.shape[1]
    cores, planes = received_ref.shape[:2]

    @pl.when(is_first)
    def _():
        x_ref[...] = entering_ref[...]

    @pl.when(jnp.logical_not(is_first))
    def _():
        for core in range(cores):
            for plane in range(planes):
                head = plane * cores + core
                x_ref[:, head * shard : (head + 1) * shard] = received_ref[core, plane]

    for head in range(cores * planes):

        @pl.when(where_ref[3] == head)
        def _():
            own_ref[...] = x_ref[:, head * shard : (head + 1) * shard]

    normalise(x_ref, root_mean_square(x_ref), gain_ref, normed_ref)
    row = segments_ref[pl.ds(where_ref[1], 1), :]
    ready = (lambda: None,) * 4
    attend(
        normed_ref, row, is_first, key_ref, value_ref, query_ref, scale_ref, blend_ref, earlier_ref, ready,
        attended_ref, None,
    )


def pieces_kernel(before_ref, normed_ref, cotangent_ref, pieces_ref):
    replicas = pieces_ref.shape[0]
    rows = normed_ref.shape[1] // replicas
    contract = (((1,), (0,)), ((), ()))
    first = cotangent_ref[0].astype(jnp.float32).T.astype(jnp.bfloat16)
    second = cotangent_ref[1].astype(jnp.float32).T.astype(jnp.bfloat16)
    for replica in range(replicas):
        columns = slice(replica * rows, (replica + 1) * rows)
        term = lax.dot_general(first, before_ref[:, columns], contract, preferred_element_type=jnp.float32)
        term += lax.dot_general(second, normed_ref[:, columns], contract, preferred_element_type=jnp.float32)
        pieces_ref[replica] = term.astype(jnp.bfloat16)


def total_kernel(pieces_ref, total_ref):
    total = pieces_ref[0].astype(jnp.float32)
    for replica in range(1, pieces_ref.shape[0]):
        total += pieces_ref[replica].astype(jnp.float32)
    total_ref[...] = total.T


PARAMS = pltpu.CompilerParams(vmem_limit_bytes=16 * 1024 * 1024)


def per_device(
    segments,
    section_input_stream,
    entering,
    pending_first_values,
    norm_gain_vector,
    query_weight,
    key_weight,
    value_weight,
    output_weight,
    query_key_scale,
    value_blend_weight,
    value_cotangent_rows,
):
    section_index = lax.axis_index("section")
    head_index = lax.axis_index("head")
    is_first = section_index == 0
    width = output_weight.shape[1]
    shard_width = output_weight.shape[2]
    total_batches, tokens = segments.shape
    kv_width = key_weight.shape[2]
    replicas = lax.axis_size("dp")
    grad_rows = width // replicas
    query_proj = query_weight[0]
    key_proj = key_weight[0]
    value_proj = value_weight[0]
    out_proj = output_weight[0]
    q_width = query_proj.shape[1]
    shape = jax.ShapeDtypeStruct
    half, floats = jnp.bfloat16, jnp.float32
    slots = jnp.arange(4, dtype=jnp.int32)
    before = jnp.where(is_first, total_batches - 1, section_index - 1)
    plane = head_index // (lax.axis_size("head") // 2)
    where = jnp.where(
        slots < 2,
        jnp.where(slots == 0, section_index, before),
        jnp.where(slots == 2, plane, head_index),
    ).astype(jnp.int32)
    own_first = section_input_stream[0]

    def project(own_rows, attended):
        return (
            own_rows.astype(floats)
            + jnp.dot(collect(attended), out_proj, preferred_element_type=floats)
        ).astype(half)

    in_hbm = [
        pltpu.with_memory_space_constraint(array, pltpu.HBM)
        for array in (segments, norm_gain_vector, pending_first_values[0], key_proj, value_proj, query_proj)
    ]
    attended_first, carried_first, normed_first = pl.pallas_call(
        first_kernel,
        out_shape=(
            shape((tokens, q_width), half),
            shape((tokens, kv_width), half),
            shape((tokens, width), half),
        ),
        in_specs=[SMEM] * 3 + [VMEM] + [HBM] * 6,
        out_specs=(VMEM, VMEM, HBM),
        scratch_shapes=[pltpu.VMEM(array.shape, array.dtype) for array in in_hbm]
        + [pltpu.VMEM((tokens, width), half), pltpu.SemaphoreType.DMA((7,))],
        compiler_params=PARAMS,
        name="first_round",
    )(where, query_key_scale, value_blend_weight, collect(own_first), *in_hbm)
    output_first = project(own_first, attended_first)
    received_half = next_section(collect_planes(output_first))
    received_values = next_section(carried_first)
    attended_second, own_second, normed_second = pl.pallas_call(
        second_kernel,
        out_shape=(
            shape((tokens, q_width), half),
            shape((tokens, shard_width), half),
            shape((tokens, width), half),
        ),
        in_specs=[SMEM] * 3 + [VMEM] * 8,
        out_specs=(VMEM,) * 3,
        scratch_shapes=[pltpu.VMEM((tokens, width), half)],
        compiler_params=PARAMS,
        name="second_round",
    )(
        where, query_key_scale, value_blend_weight, collect_chip(received_half), entering, segments, norm_gain_vector,
        received_values, key_proj, value_proj, query_proj,
    )
    pieces = pl.pallas_call(
        pieces_kernel,
        out_shape=shape((replicas, kv_width, grad_rows), half),
        in_specs=[VMEM] * 3,
        out_specs=VMEM,
        compiler_params=PARAMS,
        name="pieces",
    )(normed_first, normed_second, value_cotangent_rows[0])
    exchanged = lax.all_to_all(pieces, "dp", 0, 0, tiled=True)
    output_second = project(own_second, attended_second)
    gradients = pl.pallas_call(
        total_kernel,
        out_shape=shape((grad_rows, kv_width), floats),
        in_specs=[VMEM],
        out_specs=VMEM,
        compiler_params=PARAMS,
        name="gradient_total",
    )(exchanged)
    return (output_first[None], output_second[None], gradients[None])


def solution(mesh):
    return jax.shard_map(
        per_device,
        mesh=mesh,
        in_specs=(
            P(None, "dp"),
            P("section", "dp", "head"),
            P("dp", None),
            P("section", "dp", "head"),
            P("section", None),
            P("section", None, "head"),
            P("section", None, "head"),
            P("section", None, "head"),
            P("section", None, "head"),
            P("section", "head"),
            P("section", "head"),
            P("section", None, "dp", "head"),
        ),
        out_specs=(
            P("section", "dp", "head"),
            P("section", "dp", "head"),
            P("section", "dp", "head"),
        ),
        check_vma=False,
    )
```

time: 193 us -> 188 us (0.974)
  the two profiles are of different devices: /device:TPU:931 before, /device:TPU:449 now
where the time goes in v2:
time: 188 us
  blocking collectives  158 us (84%)
  Pallas kernels  10.9 us (6%)
  starting transfers between devices  10.1 us (5%)
  waiting for transfers between devices  5.14 us (3%)
    all_gather x3, blocking collectives, collect(): return lax.all_gather(piece, 'head', axis=1, tiled=True)  114 us
    all_gather x1, blocking collectives, collect_planes(): return lax.all_gather(piece, 'head', axis_index_groups=pairs)  40.3 us
    all_to_all x1, starting transfers between devices, per_device(): exchanged = lax.all_to_all(pieces, 'dp', 0, 0, tiled=True)  6.3 us
    ppermute x2, waiting for transfers between devices, next_section(): lax.ppermute(piece, 'section', [(i, i + 1) for i in range(peers - 1)])  5.14 us
    pallas_call x1, Pallas kernels, per_device(): pl.pallas_call(first_kernel, out_shape=(shape((tokens, q_width), half), s...  5.12 us
    ppermute x2, starting transfers between devices, next_section(): lax.ppermute(piece, 'section', [(i, i + 1) for i in range(peers - 1)])  3.83 us
    all_gather x1, blocking collectives, collect_chip(): return lax.all_gather(piece, 'head', axis_index_groups=chips)  3.77 us
  transfers between devices with their start and end apart: 3, of which 1 were waited for; matrix products, arithmetic and copies ran while one was open for 1% of the time, Pallas kernels for 0%

profile of v2, /device:TPU:449, one launch (start us, length us, event | category | flops | bytes accessed | tf_op | source)
XLA Modules:
  0.0 188.0 jit_solution(11833648795656088183)
XLA Ops:
  0.6 0.0 copy-start
  1.5 42.8 %all-gather = bf16[1,128,2048]{2,1,0:T(8,128)(2,1)S(1)} all-gather(bf16[1,128,512]{2,1,0:T(8,128)(2,1)} %param.13), channel_id=2, replica_groups=mesh['section'=16,'dp'=16,'head'=4] {'head'}, dimensions={2}, use_global_device_ids=true | all-gather | bytes 655360 | tf_op jit(solution)/shard_map/all_gather | solution.py:20
  44.3 0.0 copy-start.8
  44.3 0.7 copy-done.8
  44.9 0.0 copy-start.9
  44.9 5.1 %first_round.1 = (bf16[128,512]{1,0:T(8,128)(2,1)S(1)}, bf16[128,128]{1,0:T(8,128)(2,1)S(1)}, bf16[128,2048]{1,0:T(8,128)(2,1)S(1)}) custom-call(s32[4]{0:T(128)S(1)} %compare_select_fusion.2.where_ref, f32[1,4]{1,0:T(1,128)S(1)} %copy-done.8, f32[1,1]{1,0:T(1,128)S(6)} %copy.15.blend_ref, bf16[128,2048]{1,0:T(8,128)(2,1)S(1)} %bitcast.35, ...), custom_call_target="tpu_custom_call" | custom-call | tf_op jit(solution)/shard_map/first_round/pallas_call | solution.py:251
  50.0 30.9 %all_gather.20 = bf16[128,2048]{1,0:T(8,128)(2,1)S(1)} all-gather(bf16[128,512]{1,0:T(8,128)(2,1)S(1)} %get-tuple-element.9), channel_id=1, replica_groups=mesh['section'=16,'dp'=16,'head'=4] {'head'}, dimensions={1}, use_global_device_ids=true | all-gather | bytes 655360 | tf_op jit(solution)/shard_map/all_gather | solution.py:20
  81.0 0.0 copy-done
  81.0 0.0 copy-done.9
  81.0 0.0 copy-start.1
  81.0 0.0 copy-start.2
  81.0 0.0 copy-start.3
  81.0 0.0 copy-start.4
  81.0 0.0 copy-start.6
  81.0 0.0 copy-start.7
  81.1 0.5 fusion.7
  81.5 0.0 copy-start.10
  81.5 40.3 %all-gather.1 = bf16[256,512]{1,0:T(8,128)(2,1)S(1)} all-gather(bf16[128,512]{1,0:T(8,128)(2,1)S(1)} %fusion.7), channel_id=3, replica_groups={{0,2},{1,3},{4,6},{5,7},{8,10},{9,11},{12,14},{13,15},{16,18},{17,19},{..., dimensions={0}, use_global_device_ids=true | all-gather | bytes 393216 | tf_op jit(solution)/shard_map/all_gather | solution.py:32
  121.8 1.9 %collective-permute-start = (bf16[2,128,512]{2,1,0:T(8,128)(2,1)S(1)}, bf16[2,128,512]{2,1,0:T(8,128)(2,1)S(1)}, u32[]{:S(2)}, u32[]{:S(2)}) collective-permute-start(bf16[2,128,512]{2,1,0:T(8,128)(2,1)S(1)} %bitcast.38), channel_id=1, source_target_pairs={{0,64},{64,128},{128,192},{192,256},{256,320},{320,384},{384,448},... | collective-permute-start | bytes 786440 | tf_op jit(solution)/shard_map/ppermute | solution.py:37
  123.8 1.9 %collective-permute-start.1 = (bf16[128,128]{1,0:T(8,128)(2,1)S(1)}, bf16[128,128]{1,0:T(8,128)(2,1)S(1)}, u32[]{:S(2)}, u32[]{:S(2)}) collective-permute-start(bf16[128,128]{1,0:T(8,128)(2,1)S(1)} %get-tuple-element.10), channel_id=1, source_target_pairs={{0,64},{64,128},{128,192},{192,256},{256,320},{320,384},{384,448},... | collective-permute-start | bytes 98312 | tf_op jit(solution)/shard_map/ppermute | solution.py:37
  125.7 5.1 %collective-permute-done = bf16[2,128,512]{2,1,0:T(8,128)(2,1)S(1)} collective-permute-done((bf16[2,128,512]{2,1,0:T(8,128)(2,1)S(1)}, bf16[2,128,512]{2,1,0:T(8,128)(2,1)S(1)}, u32[]{:S(2)}, u32[]{:S(2)}) %collective-permute-start) | collective-permute-done | bytes 262176 | tf_op jit(solution)/shard_map/ppermute | solution.py:37
  130.8 3.8 %all-gather.2 = bf16[4,128,512]{2,1,0:T(8,128)(2,1)S(1)} all-gather(bf16[2,128,512]{2,1,0:T(8,128)(2,1)S(1)} %collective-permute-done), channel_id=4, replica_groups={{0,1},{2,3},{4,5},{6,7},{8,9},{10,11},{12,13},{14,15},{16,17},{18,19},{..., dimensions={0}, use_global_device_ids=true | all-gather | bytes 786432 | tf_op jit(solution)/shard_map/all_gather | solution.py:26
  134.6 0.0 collective-permute-done.1.earlier_ref
  134.6 0.0 copy-done.1
  134.6 0.0 copy-done.2
  134.6 0.0 copy-done.3
  134.6 0.0 copy-done.4
  134.6 0.0 copy-done.6
  134.6 0.0 copy-done.7
  134.6 0.0 copy-start.5
  134.6 3.7 %second_round.1 = (bf16[128,512]{1,0:T(8,128)(2,1)S(1)}, bf16[128,512]{1,0:T(8,128)(2,1)S(1)}, bf16[128,2048]{1,0:T(8,128)(2,1)S(1)}) custom-call(s32[4]{0:T(128)S(1)} %compare_select_fusion.2.where_ref, f32[1,4]{1,0:T(1,128)S(1)} %copy-done.8, f32[1,1]{1,0:T(1,128)S(6)} %copy.15.blend_ref, bf16[2,2,128,512]{3,2,1,0:T(8,128)(2,1)S(1)} %bitcast.30, ...), custom_call_target="tpu_custom_call" | custom-call | tf_op jit(solution)/shard_map/second_round/pallas_call | solution.py:268
  138.3 0.0 copy-done.10
  138.3 0.0 copy-done.5
  138.3 1.3 pieces.1
  139.7 6.3 %all-to-all-start = ((bf16[16,128,128]{2,1,0:T(8,128)(2,1)}), bf16[16,128,128]{2,1,0:T(8,128)(2,1)S(1)}, u32[]{:S(2)}, u32[]{:S(2)}) async-start(bf16[16,128,128]{2,1,0:T(8,128)(2,1)} %pieces.1), calls=%async_computation | async-start | bytes 1048576 | tf_op jit(solution)/shard_map/all_to_all | solution.py:292
  146.0 40.2 %all_gather.24 = bf16[128,2048]{1,0:T(8,128)(2,1)S(1)} all-gather(bf16[128,512]{1,0:T(8,128)(2,1)S(1)} %get-tuple-element.12), channel_id=1, replica_groups=mesh['section'=16,'dp'=16,'head'=4] {'head'}, dimensions={1}, use_global_device_ids=true | all-gather | bytes 655360 | tf_op jit(solution)/shard_map/all_gather | solution.py:20
  186.1 1.1 fusion.10
  187.2 0.0 all-to-all-done.pieces_ref
  187.2 0.8 gradient_total.1
  (1 shorter events, 0.0 us)
Async XLA Ops:
  0.6 80.4 %copy-start = (bf16[1,2048,512]{2,1,0:T(8,128)(2,1)S(1)}, bf16[1,2048,512]{2,1,0:T(8,128)(2,1)}, u32[]{:S(2)}) copy-start(bf16[1,2048,512]{2,1,0:T(8,128)(2,1)} %param.20) | copy-start | bytes 6291460
  44.3 0.7 copy-start.8
  44.9 36.1 %copy-start.9 = (bf16[1,128,512]{2,1,0:T(8,128)(2,1)S(1)}, bf16[1,128,512]{2,1,0:T(8,128)(2,1)}, u32[]{:S(2)}) copy-start(bf16[1,128,512]{2,1,0:T(8,128)(2,1)} %param.13) | copy-start | bytes 393220
  81.0 53.6 %copy-start.1 = (bf16[1,2048,512]{2,1,0:T(8,128)(2,1)S(1)}, bf16[1,2048,512]{2,1,0:T(8,128)(2,1)}, u32[]{:S(2)}) copy-start(bf16[1,2048,512]{2,1,0:T(8,128)(2,1)} %param.17) | copy-start | bytes 6291460
  81.0 53.6 %copy-start.2 = (bf16[1,2048,128]{2,1,0:T(8,128)(2,1)S(1)}, bf16[1,2048,128]{2,1,0:T(8,128)(2,1)}, u32[]{:S(2)}) copy-start(bf16[1,2048,128]{2,1,0:T(8,128)(2,1)} %param.18) | copy-start | bytes 1572868
  81.0 53.6 %copy-start.3 = (bf16[1,2048,128]{2,1,0:T(8,128)(2,1)S(1)}, bf16[1,2048,128]{2,1,0:T(8,128)(2,1)}, u32[]{:S(2)}) copy-start(bf16[1,2048,128]{2,1,0:T(8,128)(2,1)} %param.19) | copy-start | bytes 1572868
  81.0 53.6 %copy-start.4 = (bf16[128,2048]{1,0:T(8,128)(2,1)S(1)}, bf16[128,2048]{1,0:T(8,128)(2,1)}, u32[]{:S(2)}) copy-start(bf16[128,2048]{1,0:T(8,128)(2,1)} %entering_ref.1) | copy-start | bytes 1572868
  81.0 53.6 %copy-start.6 = (s32[17,128]{1,0:T(8,128)S(1)}, s32[17,128]{1,0:T(8,128)}, u32[]{:S(2)}) copy-start(s32[17,128]{1,0:T(8,128)} %segments_ref.1) | copy-start | bytes 26116
  81.0 53.6 %copy-start.7 = (f32[1,2048]{1,0:T(1,128)S(1)}, f32[1,2048]{1,0:T(1,128)}, u32[]{:S(2)}) copy-start(f32[1,2048]{1,0:T(1,128)} %gain_ref.1) | copy-start | bytes 24580
  81.5 56.8 %copy-start.10 = (bf16[128,512]{1,0:T(8,128)(2,1)}, bf16[128,512]{1,0:T(8,128)(2,1)S(1)}, u32[]{:S(2)}) copy-start(bf16[128,512]{1,0:T(8,128)(2,1)S(1)} %fusion.7) | copy-start | bytes 393220
  121.8 9.0 %collective-permute-start = (bf16[2,128,512]{2,1,0:T(8,128)(2,1)S(1)}, bf16[2,128,512]{2,1,0:T(8,128)(2,1)S(1)}, u32[]{:S(2)}, u32[]{:S(2)}) collective-permute-start(bf16[2,128,512]{2,1,0:T(8,128)(2,1)S(1)} %bitcast.38), channel_id=1, source_target_pairs={{0,64},{64,128},{128,192},{192,256},{256,320},{320,384},{384,448},... | collective-permute-start | bytes 786440 | tf_op jit(solution)/shard_map/ppermute | solution.py:37
  123.8 10.8 %collective-permute-start.1 = (bf16[128,128]{1,0:T(8,128)(2,1)S(1)}, bf16[128,128]{1,0:T(8,128)(2,1)S(1)}, u32[]{:S(2)}, u32[]{:S(2)}) collective-permute-start(bf16[128,128]{1,0:T(8,128)(2,1)S(1)} %get-tuple-element.10), channel_id=1, source_target_pairs={{0,64},{64,128},{128,192},{192,256},{256,320},{320,384},{384,448},... | collective-permute-start | bytes 98312 | tf_op jit(solution)/shard_map/ppermute | solution.py:37
  134.6 3.7 %copy-start.5 = (bf16[1,2,128,128]{3,2,1,0:T(8,128)(2,1)S(1)}, bf16[1,2,128,128]{3,2,1,0:T(8,128)(2,1)}, u32[]{:S(2)}) copy-start(bf16[1,2,128,128]{3,2,1,0:T(8,128)(2,1)} %param.23) | copy-start | bytes 196612
  139.7 47.6 %all-to-all-start = ((bf16[16,128,128]{2,1,0:T(8,128)(2,1)}), bf16[16,128,128]{2,1,0:T(8,128)(2,1)S(1)}, u32[]{:S(2)}, u32[]{:S(2)}) async-start(bf16[16,128,128]{2,1,0:T(8,128)(2,1)} %pieces.1), calls=%async_computation | async-start | bytes 1048576 | tf_op jit(solution)/shard_map/all_to_all | solution.py:292

commit v3 on v2

--- a/solution.py
+++ b/solution.py
@@ -30,6 +30,11 @@
     peers = lax.axis_size("head")
     pairs = [[i, i + peers // 2] for i in range(peers // 2)]
     return lax.all_gather(piece, "head", axis_index_groups=pairs)
+
+
+def swap_planes(piece):
+    peers = lax.axis_size("head")
+    return lax.ppermute(piece, "head", [(i, (i + peers // 2) % peers) for i in range(peers)])
 
 
 def next_section(piece):
@@ -110,17 +115,18 @@
 
 
 def first_kernel(
-    where_ref, scale_ref, blend_ref, x_ref, segments_in, gain_in, earlier_in, key_in, value_in, query_in,
+    where_ref, blend_ref, x_ref, segments_in, gain_in, scale_in, earlier_in, key_in, value_in, query_in,
     attended_ref, carried_ref, normed_out,
-    segments_ref, gain_ref, earlier_ref, key_ref, value_ref, query_ref, normed_ref, semaphores,
-):
-    gain, segments, key, value, earlier, query = begin(
+    segments_ref, gain_ref, scale_ref, earlier_ref, key_ref, value_ref, query_ref, normed_ref, semaphores,
+):
+    gain, segments, scale, earlier, key, value, query = begin(
         [
             (gain_in, gain_ref),
             (segments_in, segments_ref),
+            (scale_in, scale_ref),
+            (earlier_in, earlier_ref),
             (key_in, key_ref),
             (value_in, value_ref),
-            (earlier_in, earlier_ref),
             (query_in, query_ref),
         ],
         semaphores,
@@ -128,9 +134,10 @@
     root = root_mean_square(x_ref)
     gain.wait()
     normalise(x_ref, root, gain_ref, normed_ref)
-    normed_copy = pltpu.make_async_copy(normed_ref, normed_out, semaphores.at[6])
+    normed_copy = pltpu.make_async_copy(normed_ref, normed_out, semaphores.at[7])
     normed_copy.start()
     segments.wait()
+    scale.wait()
     row = segments_ref[pl.ds(where_ref[0], 1), :]
     attend(
         normed_ref, row, where_ref[0] == 0, key_ref, value_ref, query_ref, scale_ref, blend_ref, earlier_ref,
@@ -139,43 +146,7 @@
     normed_copy.wait()
 
 
-def second_kernel(
-    where_ref, scale_ref, blend_ref, received_ref, entering_ref, segments_ref, gain_ref, earlier_ref, key_ref,
-    value_ref, query_ref,
-    attended_ref, own_ref, normed_ref,
-    x_ref,
-):
-    is_first = where_ref[0] == 0
-    shard = own_ref.shape[1]
-    cores, planes = received_ref.shape[:2]
-
-    @pl.when(is_first)
-    def _():
-        x_ref[...] = entering_ref[...]
-
-    @pl.when(jnp.logical_not(is_first))
-    def _():
-        for core in range(cores):
-            for plane in range(planes):
-                head = plane * cores + core
-                x_ref[:, head * shard : (head + 1) * shard] = received_ref[core, plane]
-
-    for head in range(cores * planes):
-
-        @pl.when(where_ref[3] == head)
-        def _():
-            own_ref[...] = x_ref[:, head * shard : (head + 1) * shard]
-
-    normalise(x_ref, root_mean_square(x_ref), gain_ref, normed_ref)
-    row = segments_ref[pl.ds(where_ref[1], 1), :]
-    ready = (lambda: None,) * 4
-    attend(
-        normed_ref, row, is_first, key_ref, value_ref, query_ref, scale_ref, blend_ref, earlier_ref, ready,
-        attended_ref, None,
-    )
-
-
-def pieces_kernel(before_ref, normed_ref, cotangent_ref, pieces_ref):
+def gradient_pieces(before_ref, normed_ref, cotangent_ref, pieces_ref):
     replicas = pieces_ref.shape[0]
     rows = normed_ref.shape[1] // replicas
     contract = (((1,), (0,)), ((), ()))
@@ -188,10 +159,63 @@
         pieces_ref[replica] = term.astype(jnp.bfloat16)
 
 
-def total_kernel(pieces_ref, total_ref):
-    total = pieces_ref[0].astype(jnp.float32)
-    for replica in range(1, pieces_ref.shape[0]):
-        total += pieces_ref[replica].astype(jnp.float32)
+def second_kernel(
+    where_ref, blend_ref, scale_in, received_ref, entering_ref, segments_ref, gain_ref, earlier_ref, key_ref,
+    value_ref, query_ref, before_ref, cotangent_ref,
+    attended_ref, own_ref, pieces_out,
+    scale_ref, x_ref, normed_ref, pieces_ref, semaphores,
+):
+    (scale,) = begin([(scale_in, scale_ref)], semaphores)
+    is_first = where_ref[0] == 0
+    shard = own_ref.shape[1]
+    cores, planes = received_ref.shape[:2]
+
+    @pl.when(is_first)
+    def _():
+        x_ref[...] = entering_ref[...]
+
+    @pl.when(jnp.logical_not(is_first))
+    def _():
+        for core in range(cores):
+            for plane in range(planes):
+                head = plane * cores + core
+                x_ref[:, head * shard : (head + 1) * shard] = received_ref[core, plane]
+
+    for head in range(cores * planes):
+
+        @pl.when(where_ref[3] == head)
+        def _():
+            own_ref[...] = x_ref[:, head * shard : (head + 1) * shard]
+
+    normalise(x_ref, root_mean_square(x_ref), gain_ref, normed_ref)
+    gradient_pieces(before_ref, normed_ref, cotangent_ref, pieces_ref)
+    pieces_copy = pltpu.make_async_copy(pieces_ref, pieces_out, semaphores.at[1])
+    pieces_copy.start()
+    scale.wait()
+    row = segments_ref[pl.ds(where_ref[1], 1), :]
+    ready = (lambda: None,) * 4
+    attend(
+        normed_ref, row, is_first, key_ref, value_ref, query_ref, scale_ref, blend_ref, earlier_ref, ready,
+        attended_ref, None,
+    )
+    pieces_copy.wait()
+
+
+def last_kernel(
+    where_ref, near_ref, far_ref, weight_ref, own_ref, exchanged_in, out_ref, total_ref, exchanged_ref, semaphores
+):
+    (exchanged,) = begin([(exchanged_in, exchanged_ref)], semaphores)
+    product = own_ref[...].astype(jnp.float32)
+    cores, _, width = near_ref.shape
+    for side_ref, plane in ((near_ref, where_ref[2]), (far_ref, 1 - where_ref[2])):
+        for core in range(cores):
+            start = pl.multiple_of((plane * cores + core) * width, width)
+            product += jnp.dot(side_ref[core], weight_ref[pl.ds(start, width), :], preferred_element_type=jnp.float32)
+    out_ref[...] = product.astype(jnp.bfloat16)
+    exchanged.wait()
+    total = exchanged_ref[0].astype(jnp.float32)
+    for replica in range(1, exchanged_ref.shape[0]):
+        total += exchanged_ref[replica].astype(jnp.float32)
     total_ref[...] = total.T
 
 
@@ -246,7 +270,10 @@
 
     in_hbm = [
         pltpu.with_memory_space_constraint(array, pltpu.HBM)
-        for array in (segments, norm_gain_vector, pending_first_values[0], key_proj, value_proj, query_proj)
+        for array in (
+            segments, norm_gain_vector, query_key_scale, pending_first_values[0], key_proj,
+            value_proj, query_proj,
+        )
     ]
     attended_first, carried_first, normed_first = pl.pallas_call(
         first_kernel,
@@ -255,50 +282,56 @@
             shape((tokens, kv_width), half),
             shape((tokens, width), half),
         ),
-        in_specs=[SMEM] * 3 + [VMEM] + [HBM] * 6,
+        in_specs=[SMEM, SMEM, VMEM] + [HBM] * 7,
         out_specs=(VMEM, VMEM, HBM),
-        scratch_shapes=[pltpu.VMEM(array.shape, array.dtype) for array in in_hbm]
-        + [pltpu.VMEM((tokens, width), half), pltpu.SemaphoreType.DMA((7,))],
+        scratch_shapes=[
+            (pltpu.SMEM if array.size < LANES else pltpu.VMEM)(array.shape, array.dtype) for array in in_hbm
+        ]
+        + [pltpu.VMEM((tokens, width), half), pltpu.SemaphoreType.DMA((8,))],
         compiler_params=PARAMS,
         name="first_round",
-    )(where, query_key_scale, value_blend_weight, collect(own_first), *in_hbm)
+    )(where, value_blend_weight, collect(own_first), *in_hbm)
     output_first = project(own_first, attended_first)
     received_half = next_section(collect_planes(output_first))
     received_values = next_section(carried_first)
-    attended_second, own_second, normed_second = pl.pallas_call(
+    attended_second, own_second, pieces = pl.pallas_call(
         second_kernel,
         out_shape=(
             shape((tokens, q_width), half),
             shape((tokens, shard_width), half),
-            shape((tokens, width), half),
+            shape((replicas, kv_width, grad_rows), half),
         ),
-        in_specs=[SMEM] * 3 + [VMEM] * 8,
-        out_specs=(VMEM,) * 3,
-        scratch_shapes=[pltpu.VMEM((tokens, width), half)],
+        in_specs=[SMEM, SMEM, HBM] + [VMEM] * 10,
+        out_specs=(VMEM, VMEM, HBM),
+        scratch_shapes=[
+            pltpu.SMEM(query_key_scale.shape, floats),
+            pltpu.VMEM((tokens, width), half),
+            pltpu.VMEM((tokens, width), half),
+            pltpu.VMEM((replicas, kv_width, grad_rows), half),
+            pltpu.SemaphoreType.DMA((2,)),
+        ],
         compiler_params=PARAMS,
         name="second_round",
     )(
-        where, query_key_scale, value_blend_weight, collect_chip(received_half), entering, segments, norm_gain_vector,
-        received_values, key_proj, value_proj, query_proj,
-    )
-    pieces = pl.pallas_call(
-        pieces_kernel,
-        out_shape=shape((replicas, kv_width, grad_rows), half),
-        in_specs=[VMEM] * 3,
-        out_specs=VMEM,
+        where, value_blend_weight, in_hbm[2], collect_chip(received_half), entering, segments, norm_gain_vector,
+        received_values, key_proj, value_proj, query_proj, normed_first, value_cotangent_rows[0],
+    )
+    across = swap_planes(attended_second)
+    near = collect_chip(attended_second)
+
+    once = lax.optimization_barrier(jnp.int32(1))
+    exchanged = lax.fori_loop(0, once, lambda _, sent: lax.all_to_all(sent, "dp", 0, 0, tiled=True), pieces)
+    across, near, exchanged = lax.optimization_barrier((across, near, exchanged))
+    far = collect_chip(across)
+    output_second, gradients = pl.pallas_call(
+        last_kernel,
+        out_shape=(shape((tokens, shard_width), half), shape((grad_rows, kv_width), floats)),
+        in_specs=[SMEM] + [VMEM] * 4 + [HBM],
+        out_specs=(VMEM, VMEM),
+        scratch_shapes=[pltpu.VMEM(exchanged.shape, half), pltpu.SemaphoreType.DMA((1,))],
         compiler_params=PARAMS,
-        name="pieces",
-    )(normed_first, normed_second, value_cotangent_rows[0])
-    exchanged = lax.all_to_all(pieces, "dp", 0, 0, tiled=True)
-    output_second = project(own_second, attended_second)
-    gradients = pl.pallas_call(
-        total_kernel,
-        out_shape=shape((grad_rows, kv_width), floats),
-        in_specs=[VMEM],
-        out_specs=VMEM,
-        compiler_params=PARAMS,
-        name="gradient_total",
-    )(exchanged)
+        name="last",
+    )(where, near, far, out_proj, own_second, pltpu.with_memory_space_constraint(exchanged, pltpu.HBM))
     return (output_first[None], output_second[None], gradients[None])
 
 

time: 188 us -> 183 us (0.973)
  blocking collectives: 158 us -> 122 us
  waiting for transfers between devices: 5.14 us -> 29.7 us
  starting transfers between devices: 10.1 us -> 16.4 us
    all_gather x3 -> x2, blocking collectives: 114 us -> 73.8 us  [collect(): return lax.all_gather(piece, 'head', axis=1, tiled=True)]
    ppermute x0 -> x1, waiting for transfers between devices: none -> 14 us  [swap_planes(): lax.ppermute(piece, 'head', [(i, (i + peers // 2) % peers) for i in range...]
    all_to_all x1, waiting for transfers between devices: 0.01 us -> 10.6 us  [per_device(): lax.all_to_all(sent, 'dp', 0, 0, tiled=True)]
    ppermute x0 -> x1, starting transfers between devices: none -> 7.24 us  [swap_planes(): lax.ppermute(piece, 'head', [(i, (i + peers // 2) % peers) for i in range...]
    all_gather x1 -> x3, blocking collectives: 3.77 us -> 8.15 us  [collect_chip(): return lax.all_gather(piece, 'head', axis_index_groups=chips)]
  transfers between devices with their start and end apart: 3 -> 4, of which waited for: 1 -> 3; matrix products, arithmetic and copies ran while one was open for 1% -> 0% of each run, Pallas kernels for 0% -> 0%
where the time goes in v3:
time: 183 us
  blocking collectives  122 us (67%)
  waiting for transfers between devices  29.7 us (16%)
  starting transfers between devices  16.4 us (9%)
  Pallas kernels  11.8 us (6%)
    all_gather x2, blocking collectives, collect(): return lax.all_gather(piece, 'head', axis=1, tiled=True)  73.8 us
    all_gather x1, blocking collectives, collect_planes(): return lax.all_gather(piece, 'head', axis_index_groups=pairs)  40.2 us
    ppermute x1, waiting for transfers between devices, swap_planes(): lax.ppermute(piece, 'head', [(i, (i + peers // 2) % peers) for i in range...  14 us
    all_to_all x1, waiting for transfers between devices, per_device(): lax.all_to_all(sent, 'dp', 0, 0, tiled=True)  10.6 us
    all_gather x3, blocking collectives, collect_chip(): return lax.all_gather(piece, 'head', axis_index_groups=chips)  8.15 us
    ppermute x1, starting transfers between devices, swap_planes(): lax.ppermute(piece, 'head', [(i, (i + peers // 2) % peers) for i in range...  7.24 us
    all_to_all x1, starting transfers between devices, per_device(): lax.all_to_all(sent, 'dp', 0, 0, tiled=True)  5.29 us
    pallas_call x1, Pallas kernels, per_device(): pl.pallas_call(first_kernel, out_shape=(shape((tokens, q_width), half), s...  5.24 us
  transfers between devices with their start and end apart: 4, of which 3 were waited for; matrix products, arithmetic and copies ran while one was open for 0% of the time, Pallas kernels for 0%

profile of v3, /device:TPU:449, one launch (start us, length us, event | category | flops | bytes accessed | tf_op | source)
XLA Modules:
  0.0 182.8 jit_solution(12770434897567146583)
XLA Ops:
  1.3 42.8 %all-gather = bf16[1,128,2048]{2,1,0:T(8,128)(2,1)S(1)} all-gather(bf16[1,128,512]{2,1,0:T(8,128)(2,1)} %param.15), channel_id=2, replica_groups=mesh['section'=16,'dp'=16,'head'=4] {'head'}, dimensions={2}, use_global_device_ids=true | all-gather | bytes 655360 | tf_op jit(solution)/shard_map/all_gather | solution.py:20
  44.1 0.0 copy-start.1
  44.1 0.0 copy-start.8
  44.1 5.2 %first_round.1 = (bf16[128,512]{1,0:T(8,128)(2,1)S(1)}, bf16[128,128]{1,0:T(8,128)(2,1)S(1)}, bf16[128,2048]{1,0:T(8,128)(2,1)S(1)}) custom-call(s32[4]{0:T(128)S(1)} %compare_select_fusion.2.where_ref, f32[1,1]{1,0:T(1,128)S(6)} %copy.22.blend_ref, bf16[128,2048]{1,0:T(8,128)(2,1)S(1)} %bitcast.28, s32[17,128]{1,0:T(8,128)} %segments_ref.1, ...), custom_call_target="tpu_custom_call" | custom-call | tf_op jit(solution)/shard_map/first_round/pallas_call | solution.py:278
  49.4 31.0 %all_gather.29 = bf16[128,2048]{1,0:T(8,128)(2,1)S(1)} all-gather(bf16[128,512]{1,0:T(8,128)(2,1)S(1)} %get-tuple-element.32), channel_id=1, replica_groups=mesh['section'=16,'dp'=16,'head'=4] {'head'}, dimensions={1}, use_global_device_ids=true | all-gather | bytes 655360 | tf_op jit(solution)/shard_map/all_gather | solution.py:20
  80.4 0.0 copy-done.1
  80.4 0.0 copy-done.8
  80.4 0.0 copy-start
  80.4 0.0 copy-start.2
  80.4 0.0 copy-start.3
  80.4 0.0 copy-start.4
  80.4 0.0 copy-start.5
  80.4 0.0 copy-start.6
  80.5 0.0 copy-start.7
  80.5 0.4 fusion
  80.9 0.0 copy-start.9
  80.9 40.2 %all-gather.1 = bf16[256,512]{1,0:T(8,128)(2,1)S(1)} all-gather(bf16[128,512]{1,0:T(8,128)(2,1)S(1)} %fusion), channel_id=3, replica_groups={{0,2},{1,3},{4,6},{5,7},{8,10},{9,11},{12,14},{13,15},{16,18},{17,19},{..., dimensions={0}, use_global_device_ids=true | all-gather | bytes 393216 | tf_op jit(solution)/shard_map/all_gather | solution.py:32
  121.2 1.9 %collective-permute-start = (bf16[2,128,512]{2,1,0:T(8,128)(2,1)S(1)}, bf16[2,128,512]{2,1,0:T(8,128)(2,1)S(1)}, u32[]{:S(2)}, u32[]{:S(2)}) collective-permute-start(bf16[2,128,512]{2,1,0:T(8,128)(2,1)S(1)} %bitcast.33), channel_id=1, source_target_pairs={{0,64},{64,128},{128,192},{192,256},{256,320},{320,384},{384,448},... | collective-permute-start | bytes 786440 | tf_op jit(solution)/shard_map/ppermute | solution.py:42
  123.1 1.9 %collective-permute-start.1 = (bf16[128,128]{1,0:T(8,128)(2,1)S(1)}, bf16[128,128]{1,0:T(8,128)(2,1)S(1)}, u32[]{:S(2)}, u32[]{:S(2)}) collective-permute-start(bf16[128,128]{1,0:T(8,128)(2,1)S(1)} %get-tuple-element.33), channel_id=1, source_target_pairs={{0,64},{64,128},{128,192},{192,256},{256,320},{320,384},{384,448},... | collective-permute-start | bytes 98312 | tf_op jit(solution)/shard_map/ppermute | solution.py:42
  125.0 5.1 %collective-permute-done = bf16[2,128,512]{2,1,0:T(8,128)(2,1)S(1)} collective-permute-done((bf16[2,128,512]{2,1,0:T(8,128)(2,1)S(1)}, bf16[2,128,512]{2,1,0:T(8,128)(2,1)S(1)}, u32[]{:S(2)}, u32[]{:S(2)}) %collective-permute-start) | collective-permute-done | bytes 262176 | tf_op jit(solution)/shard_map/ppermute | solution.py:42
  130.2 3.8 %all-gather.2 = bf16[4,128,512]{2,1,0:T(8,128)(2,1)S(1)} all-gather(bf16[2,128,512]{2,1,0:T(8,128)(2,1)S(1)} %collective-permute-done), channel_id=4, replica_groups={{0,1},{2,3},{4,5},{6,7},{8,9},{10,11},{12,13},{14,15},{16,17},{18,19},{..., dimensions={0}, use_global_device_ids=true | all-gather | bytes 786432 | tf_op jit(solution)/shard_map/all_gather | solution.py:26
  133.9 0.0 collective-permute-done.1.earlier_ref
  133.9 0.0 copy-done
  133.9 0.0 copy-done.2
  133.9 0.0 copy-done.3
  133.9 0.0 copy-done.4
  133.9 0.0 copy-done.5
  134.0 0.0 copy-done.6
  134.0 0.0 copy-done.7
  134.0 4.1 %second_round.1 = (bf16[128,512]{1,0:T(8,128)(2,1)S(1)}, bf16[128,512]{1,0:T(8,128)(2,1)S(1)}, bf16[16,128,128]{2,1,0:T(8,128)(2,1)}) custom-call(s32[4]{0:T(128)S(1)} %compare_select_fusion.2.where_ref, f32[1,1]{1,0:T(1,128)S(6)} %copy.22.blend_ref, f32[1,4]{1,0:T(1,128)} %scale_in.3, bf16[2,2,128,512]{3,2,1,0:T(8,128)(2,1)S(1)} %bitcast.23, ...), custom_call_target="tpu_custom_call" | custom-call | tf_op jit(solution)/shard_map/second_round/pallas_call | solution.py:297
  138.1 0.0 copy-done.9
  138.1 7.2 %collective-permute-start.2 = (bf16[128,512]{1,0:T(8,128)(2,1)S(1)}, bf16[128,512]{1,0:T(8,128)(2,1)S(1)}, u32[]{:S(2)}, u32[]{:S(2)}) collective-permute-start(bf16[128,512]{1,0:T(8,128)(2,1)S(1)} %get-tuple-element.35), channel_id=1, source_target_pairs={{0,2},{1,3},{2,0},{3,1},{4,6},{5,7},{6,4},{7,5},{8,10},{9,11},{10,... | collective-permute-start | bytes 393224 | tf_op jit(solution)/shard_map/ppermute | solution.py:37
  145.4 2.3 %all-gather.3 = bf16[256,512]{1,0:T(8,128)(2,1)S(1)} all-gather(bf16[128,512]{1,0:T(8,128)(2,1)S(1)} %get-tuple-element.35), channel_id=5, replica_groups={{0,1},{2,3},{4,5},{6,7},{8,9},{10,11},{12,13},{14,15},{16,17},{18,19},{..., dimensions={0}, use_global_device_ids=true | all-gather | bytes 393216 | tf_op jit(solution)/shard_map/all_gather | solution.py:26
  147.7 16.7 %while.10 = (s32[]{:T(128)}, bf16[16,128,128]{2,1,0:T(8,128)(2,1)}, s32[]{:T(128)}, s32[]{:T(128)}) while((s32[]{:T(128)}, bf16[16,128,128]{2,1,0:T(8,128)(2,1)}, s32[]{:T(128)}, s32[]{:T(128)}) %tuple.24), condition=%wide.region_1.2_spmd, body=%wide.region_0.1_spmd.sunk | while | flops 2 | bytes 2621525 | solution.py:323
  147.7 5.3 %all-to-all-start = ((bf16[16,128,128]{2,1,0:T(8,128)(2,1)}), bf16[16,128,128]{2,1,0:T(8,128)(2,1)S(1)}, u32[]{:S(2)}, u32[]{:S(2)}) async-start(bf16[16,128,128]{2,1,0:T(8,128)(2,1)} %get-tuple-element.75), calls=%async_computation | async-start | bytes 1048576 | tf_op jit(solution)/shard_map/while/body/all_to_all | solution.py:323
  153.0 10.6 %all-to-all-done = bf16[16,128,128]{2,1,0:T(8,128)(2,1)S(1)} async-done(((bf16[16,128,128]{2,1,0:T(8,128)(2,1)}), bf16[16,128,128]{2,1,0:T(8,128)(2,1)S(1)}, u32[]{:S(2)}, u32[]{:S(2)}) %all-to-all-start) | async-done | bytes 524320 | tf_op jit(solution)/shard_map/while/body/all_to_all | solution.py:323
  163.6 0.8 copy.20
  164.4 14.0 %collective-permute-done.2 = bf16[128,512]{1,0:T(8,128)(2,1)S(1)} collective-permute-done((bf16[128,512]{1,0:T(8,128)(2,1)S(1)}, bf16[128,512]{1,0:T(8,128)(2,1)S(1)}, u32[]{:S(2)}, u32[]{:S(2)}) %collective-permute-start.2) | collective-permute-done | bytes 131104 | tf_op jit(solution)/shard_map/ppermute | solution.py:37
  178.4 2.1 %all-gather.4 = bf16[256,512]{1,0:T(8,128)(2,1)S(1)} all-gather(bf16[128,512]{1,0:T(8,128)(2,1)S(1)} %collective-permute-done.2), channel_id=6, replica_groups={{0,1},{2,3},{4,5},{6,7},{8,9},{10,11},{12,13},{14,15},{16,17},{18,19},{..., dimensions={0}, use_global_device_ids=true | all-gather | bytes 393216 | tf_op jit(solution)/shard_map/all_gather | solution.py:26
  180.4 2.4 %last.1 = (bf16[128,512]{1,0:T(8,128)(2,1)}, f32[128,128]{1,0:T(8,128)}) custom-call(s32[4]{0:T(128)S(1)} %compare_select_fusion.2.where_ref, bf16[2,128,512]{2,1,0:T(8,128)(2,1)S(1)} %bitcast.29, bf16[2,128,512]{2,1,0:T(8,128)(2,1)S(1)} %bitcast.30, bf16[2048,512]{1,0:T(8,128)(2,1)S(1)} %bitcast.22, bf16[128,512]{1,0:T(8,128)(2,1)S(1)} %get-tuple-element.40.own_ref, ...), custom_call_target="tpu_custom_call" | custom-call | tf_op jit(solution)/shard_map/last/pallas_call | solution.py:326
  (1 shorter events, 0.0 us)
Async XLA Ops:
  44.1 36.3 %copy-start.1 = (bf16[1,2048,512]{2,1,0:T(8,128)(2,1)S(1)}, bf16[1,2048,512]{2,1,0:T(8,128)(2,1)}, u32[]{:S(2)}) copy-start(bf16[1,2048,512]{2,1,0:T(8,128)(2,1)} %param.22) | copy-start | bytes 6291460
  44.1 36.3 %copy-start.8 = (bf16[1,128,512]{2,1,0:T(8,128)(2,1)S(1)}, bf16[1,128,512]{2,1,0:T(8,128)(2,1)}, u32[]{:S(2)}) copy-start(bf16[1,128,512]{2,1,0:T(8,128)(2,1)} %param.15) | copy-start | bytes 393220
  80.4 53.5 %copy-start = (bf16[1,2048,512]{2,1,0:T(8,128)(2,1)S(1)}, bf16[1,2048,512]{2,1,0:T(8,128)(2,1)}, u32[]{:S(2)}) copy-start(bf16[1,2048,512]{2,1,0:T(8,128)(2,1)} %param.19) | copy-start | bytes 6291460
  80.4 53.5 %copy-start.2 = (bf16[1,2048,128]{2,1,0:T(8,128)(2,1)S(1)}, bf16[1,2048,128]{2,1,0:T(8,128)(2,1)}, u32[]{:S(2)}) copy-start(bf16[1,2048,128]{2,1,0:T(8,128)(2,1)} %param.20) | copy-start | bytes 1572868
  80.4 53.5 %copy-start.3 = (bf16[1,2048,128]{2,1,0:T(8,128)(2,1)S(1)}, bf16[1,2048,128]{2,1,0:T(8,128)(2,1)}, u32[]{:S(2)}) copy-start(bf16[1,2048,128]{2,1,0:T(8,128)(2,1)} %param.21) | copy-start | bytes 1572868
  80.4 53.5 %copy-start.4 = (bf16[128,2048]{1,0:T(8,128)(2,1)S(1)}, bf16[128,2048]{1,0:T(8,128)(2,1)}, u32[]{:S(2)}) copy-start(bf16[128,2048]{1,0:T(8,128)(2,1)} %entering_ref.1) | copy-start | bytes 1572868
  80.4 53.5 %copy-start.5 = (bf16[1,2,128,128]{3,2,1,0:T(8,128)(2,1)S(1)}, bf16[1,2,128,128]{3,2,1,0:T(8,128)(2,1)}, u32[]{:S(2)}) copy-start(bf16[1,2,128,128]{3,2,1,0:T(8,128)(2,1)} %param.25) | copy-start | bytes 196612
  80.4 53.5 %copy-start.6 = (s32[17,128]{1,0:T(8,128)S(1)}, s32[17,128]{1,0:T(8,128)}, u32[]{:S(2)}) copy-start(s32[17,128]{1,0:T(8,128)} %segments_ref.1) | copy-start | bytes 26116
  80.5 53.5 %copy-start.7 = (f32[1,2048]{1,0:T(1,128)S(1)}, f32[1,2048]{1,0:T(1,128)}, u32[]{:S(2)}) copy-start(f32[1,2048]{1,0:T(1,128)} %gain_ref.1) | copy-start | bytes 24580
  80.9 57.2 %copy-start.9 = (bf16[128,512]{1,0:T(8,128)(2,1)}, bf16[128,512]{1,0:T(8,128)(2,1)S(1)}, u32[]{:S(2)}) copy-start(bf16[128,512]{1,0:T(8,128)(2,1)S(1)} %fusion) | copy-start | bytes 393220
  121.2 9.0 %collective-permute-start = (bf16[2,128,512]{2,1,0:T(8,128)(2,1)S(1)}, bf16[2,128,512]{2,1,0:T(8,128)(2,1)S(1)}, u32[]{:S(2)}, u32[]{:S(2)}) collective-permute-start(bf16[2,128,512]{2,1,0:T(8,128)(2,1)S(1)} %bitcast.33), channel_id=1, source_target_pairs={{0,64},{64,128},{128,192},{192,256},{256,320},{320,384},{384,448},... | collective-permute-start | bytes 786440 | tf_op jit(solution)/shard_map/ppermute | solution.py:42
  123.1 10.8 %collective-permute-start.1 = (bf16[128,128]{1,0:T(8,128)(2,1)S(1)}, bf16[128,128]{1,0:T(8,128)(2,1)S(1)}, u32[]{:S(2)}, u32[]{:S(2)}) collective-permute-start(bf16[128,128]{1,0:T(8,128)(2,1)S(1)} %get-tuple-element.33), channel_id=1, source_target_pairs={{0,64},{64,128},{128,192},{192,256},{256,320},{320,384},{384,448},... | collective-permute-start | bytes 98312 | tf_op jit(solution)/shard_map/ppermute | solution.py:42
  138.1 40.2 %collective-permute-start.2 = (bf16[128,512]{1,0:T(8,128)(2,1)S(1)}, bf16[128,512]{1,0:T(8,128)(2,1)S(1)}, u32[]{:S(2)}, u32[]{:S(2)}) collective-permute-start(bf16[128,512]{1,0:T(8,128)(2,1)S(1)} %get-tuple-element.35), channel_id=1, source_target_pairs={{0,2},{1,3},{2,0},{3,1},{4,6},{5,7},{6,4},{7,5},{8,10},{9,11},{10,... | collective-permute-start | bytes 393224 | tf_op jit(solution)/shard_map/ppermute | solution.py:37
  147.7 15.9 %all-to-all-start = ((bf16[16,128,128]{2,1,0:T(8,128)(2,1)}), bf16[16,128,128]{2,1,0:T(8,128)(2,1)S(1)}, u32[]{:S(2)}, u32[]{:S(2)}) async-start(bf16[16,128,128]{2,1,0:T(8,128)(2,1)} %get-tuple-element.75), calls=%async_computation | async-start | bytes 1048576 | tf_op jit(solution)/shard_map/while/body/all_to_all | solution.py:323

commit v4 on v3

--- a/solution.py
+++ b/solution.py
@@ -201,22 +201,27 @@
     pieces_copy.wait()
 
 
-def last_kernel(
-    where_ref, near_ref, far_ref, weight_ref, own_ref, exchanged_in, out_ref, total_ref, exchanged_ref, semaphores
-):
+def projected(heads_ref, plane, weight_ref):
+    cores, tokens, width = heads_ref.shape
+    product = jnp.zeros((tokens, weight_ref.shape[1]), jnp.float32)
+    for core in range(cores):
+        start = pl.multiple_of((plane * cores + core) * width, width)
+        product += jnp.dot(heads_ref[core], weight_ref[pl.ds(start, width), :], preferred_element_type=jnp.float32)
+    return product
+
+
+def near_kernel(where_ref, near_ref, weight_ref, own_ref, exchanged_in, partial_ref, total_ref, exchanged_ref, semaphores):
     (exchanged,) = begin([(exchanged_in, exchanged_ref)], semaphores)
-    product = own_ref[...].astype(jnp.float32)
-    cores, _, width = near_ref.shape
-    for side_ref, plane in ((near_ref, where_ref[2]), (far_ref, 1 - where_ref[2])):
-        for core in range(cores):
-            start = pl.multiple_of((plane * cores + core) * width, width)
-            product += jnp.dot(side_ref[core], weight_ref[pl.ds(start, width), :], preferred_element_type=jnp.float32)
-    out_ref[...] = product.astype(jnp.bfloat16)
+    partial_ref[...] = own_ref[...].astype(jnp.float32) + projected(near_ref, where_ref[2], weight_ref)
     exchanged.wait()
     total = exchanged_ref[0].astype(jnp.float32)
     for replica in range(1, exchanged_ref.shape[0]):
         total += exchanged_ref[replica].astype(jnp.float32)
     total_ref[...] = total.T
+
+
+def last_kernel(where_ref, far_ref, weight_ref, partial_ref, out_ref):
+    out_ref[...] = (partial_ref[...] + projected(far_ref, 1 - where_ref[2], weight_ref)).astype(jnp.bfloat16)
 
 
 PARAMS = pltpu.CompilerParams(vmem_limit_bytes=16 * 1024 * 1024)
@@ -321,17 +326,24 @@
 
     once = lax.optimization_barrier(jnp.int32(1))
     exchanged = lax.fori_loop(0, once, lambda _, sent: lax.all_to_all(sent, "dp", 0, 0, tiled=True), pieces)
-    across, near, exchanged = lax.optimization_barrier((across, near, exchanged))
-    far = collect_chip(across)
-    output_second, gradients = pl.pallas_call(
-        last_kernel,
-        out_shape=(shape((tokens, shard_width), half), shape((grad_rows, kv_width), floats)),
-        in_specs=[SMEM] + [VMEM] * 4 + [HBM],
+    partial, gradients = pl.pallas_call(
+        near_kernel,
+        out_shape=(shape((tokens, shard_width), floats), shape((grad_rows, kv_width), floats)),
+        in_specs=[SMEM] + [VMEM] * 3 + [HBM],
         out_specs=(VMEM, VMEM),
         scratch_shapes=[pltpu.VMEM(exchanged.shape, half), pltpu.SemaphoreType.DMA((1,))],
         compiler_params=PARAMS,
+        name="near",
+    )(where, near, out_proj, own_second, pltpu.with_memory_space_constraint(exchanged, pltpu.HBM))
+    across, partial = lax.optimization_barrier((across, partial))
+    output_second = pl.pallas_call(
+        last_kernel,
+        out_shape=shape((tokens, shard_width), half),
+        in_specs=[SMEM] + [VMEM] * 3,
+        out_specs=VMEM,
+        compiler_params=PARAMS,
         name="last",
-    )(where, near, far, out_proj, own_second, pltpu.with_memory_space_constraint(exchanged, pltpu.HBM))
+    )(where, collect_chip(across), out_proj, partial)
     return (output_first[None], output_second[None], gradients[None])
 
 

time: 183 us -> 182 us (level)
  waiting for transfers between devices: 29.7 us -> 27.3 us
    ppermute x1, waiting for transfers between devices: 14 us -> 11.6 us  [swap_planes(): lax.ppermute(piece, 'head', [(i, (i + peers // 2) % peers) for i in range...]
    pallas_call x1 -> x2, Pallas kernels: 2.38 us -> 3.87 us  [the longest x1 2.36 us: per_device(): pl.pallas_call(near_kernel, out_shape=(shape((tokens, shard_width), float...]
  transfers between devices with their start and end apart: 4 -> 4, of which waited for: 3 -> 3; matrix products, arithmetic and copies ran while one was open for 0% -> 0% of each run, Pallas kernels for 0% -> 1%
where the time goes in v4:
time: 182 us
  blocking collectives  122 us (67%)
  waiting for transfers between devices  27.3 us (15%)
  starting transfers between devices  16.4 us (9%)
  Pallas kernels  13.3 us (7%)
    all_gather x2, blocking collectives, collect(): return lax.all_gather(piece, 'head', axis=1, tiled=True)  73.8 us
    all_gather x1, blocking collectives, collect_planes(): return lax.all_gather(piece, 'head', axis_index_groups=pairs)  40.2 us
    ppermute x1, waiting for transfers between devices, swap_planes(): lax.ppermute(piece, 'head', [(i, (i + peers // 2) % peers) for i in range...  11.6 us
    all_to_all x1, waiting for transfers between devices, per_device(): lax.all_to_all(sent, 'dp', 0, 0, tiled=True)  10.6 us
    all_gather x3, blocking collectives, collect_chip(): return lax.all_gather(piece, 'head', axis_index_groups=chips)  8.15 us
    ppermute x1, starting transfers between devices, swap_planes(): lax.ppermute(piece, 'head', [(i, (i + peers // 2) % peers) for i in range...  7.24 us
    all_to_all x1, starting transfers between devices, per_device(): lax.all_to_all(sent, 'dp', 0, 0, tiled=True)  5.29 us
    pallas_call x1, Pallas kernels, per_device(): pl.pallas_call(first_kernel, out_shape=(shape((tokens, q_width), half), s...  5.24 us
  transfers between devices with their start and end apart: 4, of which 3 were waited for; matrix products, arithmetic and copies ran while one was open for 0% of the time, Pallas kernels for 1%

profile of v4, /device:TPU:449, one launch (start us, length us, event | category | flops | bytes accessed | tf_op | source)
XLA Modules:
  0.0 182.0 jit_solution(3285785281405119434)
XLA Ops:
  1.3 42.8 %all-gather = bf16[1,128,2048]{2,1,0:T(8,128)(2,1)S(1)} all-gather(bf16[1,128,512]{2,1,0:T(8,128)(2,1)} %param.15), channel_id=2, replica_groups=mesh['section'=16,'dp'=16,'head'=4] {'head'}, dimensions={2}, use_global_device_ids=true | all-gather | bytes 655360 | tf_op jit(solution)/shard_map/all_gather | solution.py:20
  44.1 0.0 copy-start
  44.1 0.0 copy-start.8
  44.1 5.2 %first_round.1 = (bf16[128,512]{1,0:T(8,128)(2,1)S(1)}, bf16[128,128]{1,0:T(8,128)(2,1)S(1)}, bf16[128,2048]{1,0:T(8,128)(2,1)S(1)}) custom-call(s32[4]{0:T(128)S(1)} %compare_select_fusion.2.where_ref, f32[1,1]{1,0:T(1,128)S(6)} %copy.22.blend_ref, bf16[128,2048]{1,0:T(8,128)(2,1)S(1)} %bitcast.29, s32[17,128]{1,0:T(8,128)} %segments_ref.1, ...), custom_call_target="tpu_custom_call" | custom-call | tf_op jit(solution)/shard_map/first_round/pallas_call | solution.py:283
  49.4 31.0 %all_gather.29 = bf16[128,2048]{1,0:T(8,128)(2,1)S(1)} all-gather(bf16[128,512]{1,0:T(8,128)(2,1)S(1)} %get-tuple-element.31), channel_id=1, replica_groups=mesh['section'=16,'dp'=16,'head'=4] {'head'}, dimensions={1}, use_global_device_ids=true | all-gather | bytes 655360 | tf_op jit(solution)/shard_map/all_gather | solution.py:20
  80.4 0.0 copy-done
  80.4 0.0 copy-done.8
  80.4 0.0 copy-start.1
  80.4 0.0 copy-start.2
  80.4 0.0 copy-start.3
  80.4 0.0 copy-start.4
  80.4 0.0 copy-start.5
  80.4 0.0 copy-start.6
  80.5 0.0 copy-start.7
  80.5 0.4 fusion
  80.9 0.0 copy-start.9
  80.9 40.2 %all-gather.1 = bf16[256,512]{1,0:T(8,128)(2,1)S(1)} all-gather(bf16[128,512]{1,0:T(8,128)(2,1)S(1)} %fusion), channel_id=3, replica_groups={{0,2},{1,3},{4,6},{5,7},{8,10},{9,11},{12,14},{13,15},{16,18},{17,19},{..., dimensions={0}, use_global_device_ids=true | all-gather | bytes 393216 | tf_op jit(solution)/shard_map/all_gather | solution.py:32
  121.2 1.9 %collective-permute-start = (bf16[2,128,512]{2,1,0:T(8,128)(2,1)S(1)}, bf16[2,128,512]{2,1,0:T(8,128)(2,1)S(1)}, u32[]{:S(2)}, u32[]{:S(2)}) collective-permute-start(bf16[2,128,512]{2,1,0:T(8,128)(2,1)S(1)} %bitcast.34), channel_id=1, source_target_pairs={{0,64},{64,128},{128,192},{192,256},{256,320},{320,384},{384,448},... | collective-permute-start | bytes 786440 | tf_op jit(solution)/shard_map/ppermute | solution.py:42
  123.1 1.9 %collective-permute-start.1 = (bf16[128,128]{1,0:T(8,128)(2,1)S(1)}, bf16[128,128]{1,0:T(8,128)(2,1)S(1)}, u32[]{:S(2)}, u32[]{:S(2)}) collective-permute-start(bf16[128,128]{1,0:T(8,128)(2,1)S(1)} %get-tuple-element.32), channel_id=1, source_target_pairs={{0,64},{64,128},{128,192},{192,256},{256,320},{320,384},{384,448},... | collective-permute-start | bytes 98312 | tf_op jit(solution)/shard_map/ppermute | solution.py:42
  125.0 5.1 %collective-permute-done = bf16[2,128,512]{2,1,0:T(8,128)(2,1)S(1)} collective-permute-done((bf16[2,128,512]{2,1,0:T(8,128)(2,1)S(1)}, bf16[2,128,512]{2,1,0:T(8,128)(2,1)S(1)}, u32[]{:S(2)}, u32[]{:S(2)}) %collective-permute-start) | collective-permute-done | bytes 262176 | tf_op jit(solution)/shard_map/ppermute | solution.py:42
  130.2 3.8 %all-gather.2 = bf16[4,128,512]{2,1,0:T(8,128)(2,1)S(1)} all-gather(bf16[2,128,512]{2,1,0:T(8,128)(2,1)S(1)} %collective-permute-done), channel_id=4, replica_groups={{0,1},{2,3},{4,5},{6,7},{8,9},{10,11},{12,13},{14,15},{16,17},{18,19},{..., dimensions={0}, use_global_device_ids=true | all-gather | bytes 786432 | tf_op jit(solution)/shard_map/all_gather | solution.py:26
  133.9 0.0 collective-permute-done.1.earlier_ref
  133.9 0.0 copy-done.1
  133.9 0.0 copy-done.2
  133.9 0.0 copy-done.3
  133.9 0.0 copy-done.4
  133.9 0.0 copy-done.5
  134.0 0.0 copy-done.6
  134.0 0.0 copy-done.7
  134.0 4.1 %second_round.1 = (bf16[128,512]{1,0:T(8,128)(2,1)S(1)}, bf16[128,512]{1,0:T(8,128)(2,1)S(1)}, bf16[16,128,128]{2,1,0:T(8,128)(2,1)}) custom-call(s32[4]{0:T(128)S(1)} %compare_select_fusion.2.where_ref, f32[1,1]{1,0:T(1,128)S(6)} %copy.22.blend_ref, f32[1,4]{1,0:T(1,128)} %scale_in.3, bf16[2,2,128,512]{3,2,1,0:T(8,128)(2,1)S(1)} %bitcast.24, ...), custom_call_target="tpu_custom_call" | custom-call | tf_op jit(solution)/shard_map/second_round/pallas_call | solution.py:302
  138.1 0.0 copy-done.9
  138.1 7.2 %collective-permute-start.2 = (bf16[128,512]{1,0:T(8,128)(2,1)S(1)}, bf16[128,512]{1,0:T(8,128)(2,1)S(1)}, u32[]{:S(2)}, u32[]{:S(2)}) collective-permute-start(bf16[128,512]{1,0:T(8,128)(2,1)S(1)} %get-tuple-element.34), channel_id=1, source_target_pairs={{0,2},{1,3},{2,0},{3,1},{4,6},{5,7},{6,4},{7,5},{8,10},{9,11},{10,... | collective-permute-start | bytes 393224 | tf_op jit(solution)/shard_map/ppermute | solution.py:37
  145.4 2.3 %all-gather.3 = bf16[256,512]{1,0:T(8,128)(2,1)S(1)} all-gather(bf16[128,512]{1,0:T(8,128)(2,1)S(1)} %get-tuple-element.34), channel_id=5, replica_groups={{0,1},{2,3},{4,5},{6,7},{8,9},{10,11},{12,13},{14,15},{16,17},{18,19},{..., dimensions={0}, use_global_device_ids=true | all-gather | bytes 393216 | tf_op jit(solution)/shard_map/all_gather | solution.py:26
  147.7 16.7 %while.10 = (s32[]{:T(128)}, bf16[16,128,128]{2,1,0:T(8,128)(2,1)}, s32[]{:T(128)}, s32[]{:T(128)}) while((s32[]{:T(128)}, bf16[16,128,128]{2,1,0:T(8,128)(2,1)}, s32[]{:T(128)}, s32[]{:T(128)}) %tuple.24), condition=%wide.region_1.2_spmd, body=%wide.region_0.1_spmd.sunk | while | flops 2 | bytes 2621525 | solution.py:328
  147.7 5.3 %all-to-all-start = ((bf16[16,128,128]{2,1,0:T(8,128)(2,1)}), bf16[16,128,128]{2,1,0:T(8,128)(2,1)S(1)}, u32[]{:S(2)}, u32[]{:S(2)}) async-start(bf16[16,128,128]{2,1,0:T(8,128)(2,1)} %get-tuple-element.73), calls=%async_computation | async-start | bytes 1048576 | tf_op jit(solution)/shard_map/while/body/all_to_all | solution.py:328
  153.0 10.6 %all-to-all-done = bf16[16,128,128]{2,1,0:T(8,128)(2,1)S(1)} async-done(((bf16[16,128,128]{2,1,0:T(8,128)(2,1)}), bf16[16,128,128]{2,1,0:T(8,128)(2,1)S(1)}, u32[]{:S(2)}, u32[]{:S(2)}) %all-to-all-start) | async-done | bytes 524320 | tf_op jit(solution)/shard_map/while/body/all_to_all | solution.py:328
  163.6 0.8 copy.20
  164.4 2.4 %near.1 = (f32[128,512]{1,0:T(8,128)S(1)}, f32[128,128]{1,0:T(8,128)}) custom-call(s32[4]{0:T(128)S(1)} %compare_select_fusion.2.where_ref, bf16[2,128,512]{2,1,0:T(8,128)(2,1)S(1)} %bitcast.30, bf16[2048,512]{1,0:T(8,128)(2,1)S(1)} %bitcast.20, bf16[128,512]{1,0:T(8,128)(2,1)S(1)} %get-tuple-element.35.own_ref, ...), custom_call_target="tpu_custom_call" | custom-call | tf_op jit(solution)/shard_map/near/pallas_call | solution.py:329
  166.7 11.6 %collective-permute-done.2 = bf16[128,512]{1,0:T(8,128)(2,1)S(1)} collective-permute-done((bf16[128,512]{1,0:T(8,128)(2,1)S(1)}, bf16[128,512]{1,0:T(8,128)(2,1)S(1)}, u32[]{:S(2)}, u32[]{:S(2)}) %collective-permute-start.2) | collective-permute-done | bytes 131104 | tf_op jit(solution)/shard_map/ppermute | solution.py:37
  178.4 2.1 %all-gather.4 = bf16[256,512]{1,0:T(8,128)(2,1)S(1)} all-gather(bf16[128,512]{1,0:T(8,128)(2,1)S(1)} %collective-permute-done.2), channel_id=6, replica_groups={{0,1},{2,3},{4,5},{6,7},{8,9},{10,11},{12,13},{14,15},{16,17},{18,19},{..., dimensions={0}, use_global_device_ids=true | all-gather | bytes 393216 | tf_op jit(solution)/shard_map/all_gather | solution.py:26
  180.4 1.5 last.1
  (1 shorter events, 0.0 us)
Async XLA Ops:
  44.1 36.3 %copy-start = (bf16[1,2048,512]{2,1,0:T(8,128)(2,1)S(1)}, bf16[1,2048,512]{2,1,0:T(8,128)(2,1)}, u32[]{:S(2)}) copy-start(bf16[1,2048,512]{2,1,0:T(8,128)(2,1)} %param.22) | copy-start | bytes 6291460
  44.1 36.3 %copy-start.8 = (bf16[1,128,512]{2,1,0:T(8,128)(2,1)S(1)}, bf16[1,128,512]{2,1,0:T(8,128)(2,1)}, u32[]{:S(2)}) copy-start(bf16[1,128,512]{2,1,0:T(8,128)(2,1)} %param.15) | copy-start | bytes 393220
  80.4 53.5 %copy-start.1 = (bf16[1,2048,512]{2,1,0:T(8,128)(2,1)S(1)}, bf16[1,2048,512]{2,1,0:T(8,128)(2,1)}, u32[]{:S(2)}) copy-start(bf16[1,2048,512]{2,1,0:T(8,128)(2,1)} %param.19) | copy-start | bytes 6291460
  80.4 53.5 %copy-start.2 = (bf16[1,2048,128]{2,1,0:T(8,128)(2,1)S(1)}, bf16[1,2048,128]{2,1,0:T(8,128)(2,1)}, u32[]{:S(2)}) copy-start(bf16[1,2048,128]{2,1,0:T(8,128)(2,1)} %param.20) | copy-start | bytes 1572868
  80.4 53.5 %copy-start.3 = (bf16[1,2048,128]{2,1,0:T(8,128)(2,1)S(1)}, bf16[1,2048,128]{2,1,0:T(8,128)(2,1)}, u32[]{:S(2)}) copy-start(bf16[1,2048,128]{2,1,0:T(8,128)(2,1)} %param.21) | copy-start | bytes 1572868
  80.4 53.5 %copy-start.4 = (bf16[128,2048]{1,0:T(8,128)(2,1)S(1)}, bf16[128,2048]{1,0:T(8,128)(2,1)}, u32[]{:S(2)}) copy-start(bf16[128,2048]{1,0:T(8,128)(2,1)} %entering_ref.1) | copy-start | bytes 1572868
  80.4 53.5 %copy-start.5 = (bf16[1,2,128,128]{3,2,1,0:T(8,128)(2,1)S(1)}, bf16[1,2,128,128]{3,2,1,0:T(8,128)(2,1)}, u32[]{:S(2)}) copy-start(bf16[1,2,128,128]{3,2,1,0:T(8,128)(2,1)} %param.25) | copy-start | bytes 196612
  80.4 53.5 %copy-start.6 = (s32[17,128]{1,0:T(8,128)S(1)}, s32[17,128]{1,0:T(8,128)}, u32[]{:S(2)}) copy-start(s32[17,128]{1,0:T(8,128)} %segments_ref.1) | copy-start | bytes 26116
  80.5 53.5 %copy-start.7 = (f32[1,2048]{1,0:T(1,128)S(1)}, f32[1,2048]{1,0:T(1,128)}, u32[]{:S(2)}) copy-start(f32[1,2048]{1,0:T(1,128)} %gain_ref.1) | copy-start | bytes 24580
  80.9 57.2 %copy-start.9 = (bf16[128,512]{1,0:T(8,128)(2,1)}, bf16[128,512]{1,0:T(8,128)(2,1)S(1)}, u32[]{:S(2)}) copy-start(bf16[128,512]{1,0:T(8,128)(2,1)S(1)} %fusion) | copy-start | bytes 393220
  121.2 9.0 %collective-permute-start = (bf16[2,128,512]{2,1,0:T(8,128)(2,1)S(1)}, bf16[2,128,512]{2,1,0:T(8,128)(2,1)S(1)}, u32[]{:S(2)}, u32[]{:S(2)}) collective-permute-start(bf16[2,128,512]{2,1,0:T(8,128)(2,1)S(1)} %bitcast.34), channel_id=1, source_target_pairs={{0,64},{64,128},{128,192},{192,256},{256,320},{320,384},{384,448},... | collective-permute-start | bytes 786440 | tf_op jit(solution)/shard_map/ppermute | solution.py:42
  123.1 10.8 %collective-permute-start.1 = (bf16[128,128]{1,0:T(8,128)(2,1)S(1)}, bf16[128,128]{1,0:T(8,128)(2,1)S(1)}, u32[]{:S(2)}, u32[]{:S(2)}) collective-permute-start(bf16[128,128]{1,0:T(8,128)(2,1)S(1)} %get-tuple-element.32), channel_id=1, source_target_pairs={{0,64},{64,128},{128,192},{192,256},{256,320},{320,384},{384,448},... | collective-permute-start | bytes 98312 | tf_op jit(solution)/shard_map/ppermute | solution.py:42
  138.1 40.2 %collective-permute-start.2 = (bf16[128,512]{1,0:T(8,128)(2,1)S(1)}, bf16[128,512]{1,0:T(8,128)(2,1)S(1)}, u32[]{:S(2)}, u32[]{:S(2)}) collective-permute-start(bf16[128,512]{1,0:T(8,128)(2,1)S(1)} %get-tuple-element.34), channel_id=1, source_target_pairs={{0,2},{1,3},{2,0},{3,1},{4,6},{5,7},{6,4},{7,5},{8,10},{9,11},{10,... | collective-permute-start | bytes 393224 | tf_op jit(solution)/shard_map/ppermute | solution.py:37
  147.7 15.9 %all-to-all-start = ((bf16[16,128,128]{2,1,0:T(8,128)(2,1)}), bf16[16,128,128]{2,1,0:T(8,128)(2,1)S(1)}, u32[]{:S(2)}, u32[]{:S(2)}) async-start(bf16[16,128,128]{2,1,0:T(8,128)(2,1)} %get-tuple-element.73), calls=%async_computation | async-start | bytes 1048576 | tf_op jit(solution)/shard_map/while/body/all_to_all | solution.py:328

commit v5 on v4

--- a/solution.py
+++ b/solution.py
@@ -95,23 +95,26 @@
         carried_ref[...] = jnp.where(is_first, own, earlier)
     query_wait()
     queries = jnp.dot(normed, query_ref[...], preferred_element_type=jnp.float32)
+    stacked = rms_rows(
+        jnp.concatenate([queries[:, h * HEAD_WIDTH : (h + 1) * HEAD_WIDTH] for h in range(local_heads)])
+    )
+    products = lax.dot_general(
+        stacked,
+        keys,
+        (((1,), (1,)), ((), ())),
+        precision=lax.Precision.HIGHEST,
+        preferred_element_type=jnp.float32,
+    )
+    weights = []
+    for head in range(local_heads):
+        scores = products[head * tokens : (head + 1) * tokens] * (scale_ref[0, head] / math.sqrt(HEAD_WIDTH))
+        scores = jnp.where(allowed, scores, -jnp.inf)
+        exponent = jnp.exp(scores - jnp.max(scores, axis=-1, keepdims=True))
+        weights.append((exponent / jnp.sum(exponent, axis=-1, keepdims=True)).astype(jnp.bfloat16))
+    attended = jnp.dot(jnp.concatenate(weights), mixed, preferred_element_type=jnp.float32)
     for head in range(local_heads):
         columns = slice(head * HEAD_WIDTH, (head + 1) * HEAD_WIDTH)
-        query = rms_rows(queries[:, columns])
-        scores = lax.dot_general(
-            query,
-            keys,
-            (((1,), (1,)), ((), ())),
-            precision=lax.Precision.HIGHEST,
-            preferred_element_type=jnp.float32,
-        )
-        scores = scores * (scale_ref[0, head] / math.sqrt(HEAD_WIDTH))
-        scores = jnp.where(allowed, scores, -jnp.inf)
-        exponent = jnp.exp(scores - jnp.max(scores, axis=-1, keepdims=True))
-        weights = (exponent / jnp.sum(exponent, axis=-1, keepdims=True)).astype(jnp.bfloat16)
-        attended_ref[:, columns] = jnp.dot(
-            weights, mixed, preferred_element_type=jnp.float32
-        ).astype(jnp.bfloat16)
+        attended_ref[:, columns] = attended[head * tokens : (head + 1) * tokens].astype(jnp.bfloat16)
 
 
 def first_kernel(

time: 182 us -> 180 us (0.989)
  Pallas kernels: 13.3 us -> 10.6 us
where the time goes in v5:
time: 180 us; the launch traced here: 179 us
  blocking collectives  122 us (68%)
  waiting for transfers between devices  27.5 us (15%)
  starting transfers between devices  16.3 us (9%)
  Pallas kernels  10.6 us (6%)
    all_gather x2, blocking collectives, collect(): return lax.all_gather(piece, 'head', axis=1, tiled=True)  74.4 us
    all_gather x1, blocking collectives, collect_planes(): return lax.all_gather(piece, 'head', axis_index_groups=pairs)  39.7 us
    ppermute x1, waiting for transfers between devices, swap_planes(): lax.ppermute(piece, 'head', [(i, (i + peers // 2) % peers) for i in range...  11.8 us
    all_to_all x1, waiting for transfers between devices, per_device(): lax.all_to_all(sent, 'dp', 0, 0, tiled=True)  10.6 us
    all_gather x3, blocking collectives, collect_chip(): return lax.all_gather(piece, 'head', axis_index_groups=chips)  8.19 us
    ppermute x1, starting transfers between devices, swap_planes(): lax.ppermute(piece, 'head', [(i, (i + peers // 2) % peers) for i in range...  7.17 us
    all_to_all x1, starting transfers between devices, per_device(): lax.all_to_all(sent, 'dp', 0, 0, tiled=True)  5.25 us
    ppermute x2, waiting for transfers between devices, next_section(): lax.ppermute(piece, 'section', [(i, i + 1) for i in range(peers - 1)])  5.12 us
  transfers between devices with their start and end apart: 4, of which 3 were waited for; matrix products, arithmetic and copies ran while one was open for 0% of the time, Pallas kernels for 1%

profile of v5, /device:TPU:449, one launch (start us, length us, event | category | flops | bytes accessed | tf_op | source)
XLA Modules:
  0.0 179.3 jit_solution(579998356179640918)
XLA Ops:
  1.3 42.8 %all-gather = bf16[1,128,2048]{2,1,0:T(8,128)(2,1)S(1)} all-gather(bf16[1,128,512]{2,1,0:T(8,128)(2,1)} %param.15), channel_id=2, replica_groups=mesh['section'=16,'dp'=16,'head'=4] {'head'}, dimensions={2}, use_global_device_ids=true | all-gather | bytes 655360 | tf_op jit(solution)/shard_map/all_gather | solution.py:20
  44.1 0.0 copy-start
  44.1 0.0 copy-start.8
  44.1 3.9 %first_round.1 = (bf16[128,512]{1,0:T(8,128)(2,1)S(1)}, bf16[128,128]{1,0:T(8,128)(2,1)S(1)}, bf16[128,2048]{1,0:T(8,128)(2,1)S(1)}) custom-call(s32[4]{0:T(128)S(1)} %compare_select_fusion.2.where_ref, f32[1,1]{1,0:T(1,128)S(6)} %copy.22.blend_ref, bf16[128,2048]{1,0:T(8,128)(2,1)S(1)} %bitcast.29, s32[17,128]{1,0:T(8,128)} %segments_ref.1, ...), custom_call_target="tpu_custom_call" | custom-call | tf_op jit(solution)/shard_map/first_round/pallas_call | solution.py:286
  48.0 31.6 %all_gather.29 = bf16[128,2048]{1,0:T(8,128)(2,1)S(1)} all-gather(bf16[128,512]{1,0:T(8,128)(2,1)S(1)} %get-tuple-element.31), channel_id=1, replica_groups=mesh['section'=16,'dp'=16,'head'=4] {'head'}, dimensions={1}, use_global_device_ids=true | all-gather | bytes 655360 | tf_op jit(solution)/shard_map/all_gather | solution.py:20
  79.6 0.0 copy-done
  79.6 0.0 copy-done.8
  79.6 0.0 copy-start.1
  79.6 0.0 copy-start.2
  79.6 0.0 copy-start.3
  79.6 0.0 copy-start.4
  79.6 0.0 copy-start.5
  79.6 0.0 copy-start.6
  79.6 0.0 copy-start.7
  79.7 0.4 fusion
  80.1 0.0 copy-start.9
  80.1 39.7 %all-gather.1 = bf16[256,512]{1,0:T(8,128)(2,1)S(1)} all-gather(bf16[128,512]{1,0:T(8,128)(2,1)S(1)} %fusion), channel_id=3, replica_groups={{0,2},{1,3},{4,6},{5,7},{8,10},{9,11},{12,14},{13,15},{16,18},{17,19},{..., dimensions={0}, use_global_device_ids=true | all-gather | bytes 393216 | tf_op jit(solution)/shard_map/all_gather | solution.py:32
  119.8 1.9 %collective-permute-start = (bf16[2,128,512]{2,1,0:T(8,128)(2,1)S(1)}, bf16[2,128,512]{2,1,0:T(8,128)(2,1)S(1)}, u32[]{:S(2)}, u32[]{:S(2)}) collective-permute-start(bf16[2,128,512]{2,1,0:T(8,128)(2,1)S(1)} %bitcast.34), channel_id=1, source_target_pairs={{0,64},{64,128},{128,192},{192,256},{256,320},{320,384},{384,448},... | collective-permute-start | bytes 786440 | tf_op jit(solution)/shard_map/ppermute | solution.py:42
  121.7 1.9 %collective-permute-start.1 = (bf16[128,128]{1,0:T(8,128)(2,1)S(1)}, bf16[128,128]{1,0:T(8,128)(2,1)S(1)}, u32[]{:S(2)}, u32[]{:S(2)}) collective-permute-start(bf16[128,128]{1,0:T(8,128)(2,1)S(1)} %get-tuple-element.32), channel_id=1, source_target_pairs={{0,64},{64,128},{128,192},{192,256},{256,320},{320,384},{384,448},... | collective-permute-start | bytes 98312 | tf_op jit(solution)/shard_map/ppermute | solution.py:42
  123.6 5.1 %collective-permute-done = bf16[2,128,512]{2,1,0:T(8,128)(2,1)S(1)} collective-permute-done((bf16[2,128,512]{2,1,0:T(8,128)(2,1)S(1)}, bf16[2,128,512]{2,1,0:T(8,128)(2,1)S(1)}, u32[]{:S(2)}, u32[]{:S(2)}) %collective-permute-start) | collective-permute-done | bytes 262176 | tf_op jit(solution)/shard_map/ppermute | solution.py:42
  128.7 3.8 %all-gather.2 = bf16[4,128,512]{2,1,0:T(8,128)(2,1)S(1)} all-gather(bf16[2,128,512]{2,1,0:T(8,128)(2,1)S(1)} %collective-permute-done), channel_id=4, replica_groups={{0,1},{2,3},{4,5},{6,7},{8,9},{10,11},{12,13},{14,15},{16,17},{18,19},{..., dimensions={0}, use_global_device_ids=true | all-gather | bytes 786432 | tf_op jit(solution)/shard_map/all_gather | solution.py:26
  132.5 0.0 collective-permute-done.1.earlier_ref
  132.5 0.0 copy-done.1
  132.5 0.0 copy-done.2
  132.5 0.0 copy-done.3
  132.5 0.0 copy-done.4
  132.5 0.0 copy-done.5
  132.6 0.0 copy-done.6
  132.6 0.0 copy-done.7
  132.6 2.8 %second_round.1 = (bf16[128,512]{1,0:T(8,128)(2,1)S(1)}, bf16[128,512]{1,0:T(8,128)(2,1)S(1)}, bf16[16,128,128]{2,1,0:T(8,128)(2,1)}) custom-call(s32[4]{0:T(128)S(1)} %compare_select_fusion.2.where_ref, f32[1,1]{1,0:T(1,128)S(6)} %copy.22.blend_ref, f32[1,4]{1,0:T(1,128)} %scale_in.3, bf16[2,2,128,512]{3,2,1,0:T(8,128)(2,1)S(1)} %bitcast.24, ...), custom_call_target="tpu_custom_call" | custom-call | tf_op jit(solution)/shard_map/second_round/pallas_call | solution.py:305
  135.4 0.0 copy-done.9
  135.4 7.2 %collective-permute-start.2 = (bf16[128,512]{1,0:T(8,128)(2,1)S(1)}, bf16[128,512]{1,0:T(8,128)(2,1)S(1)}, u32[]{:S(2)}, u32[]{:S(2)}) collective-permute-start(bf16[128,512]{1,0:T(8,128)(2,1)S(1)} %get-tuple-element.34), channel_id=1, source_target_pairs={{0,2},{1,3},{2,0},{3,1},{4,6},{5,7},{6,4},{7,5},{8,10},{9,11},{10,... | collective-permute-start | bytes 393224 | tf_op jit(solution)/shard_map/ppermute | solution.py:37
  142.6 2.3 %all-gather.3 = bf16[256,512]{1,0:T(8,128)(2,1)S(1)} all-gather(bf16[128,512]{1,0:T(8,128)(2,1)S(1)} %get-tuple-element.34), channel_id=5, replica_groups={{0,1},{2,3},{4,5},{6,7},{8,9},{10,11},{12,13},{14,15},{16,17},{18,19},{..., dimensions={0}, use_global_device_ids=true | all-gather | bytes 393216 | tf_op jit(solution)/shard_map/all_gather | solution.py:26
  144.9 16.7 %while.10 = (s32[]{:T(128)}, bf16[16,128,128]{2,1,0:T(8,128)(2,1)}, s32[]{:T(128)}, s32[]{:T(128)}) while((s32[]{:T(128)}, bf16[16,128,128]{2,1,0:T(8,128)(2,1)}, s32[]{:T(128)}, s32[]{:T(128)}) %tuple.24), condition=%wide.region_1.2_spmd, body=%wide.region_0.1_spmd.sunk | while | flops 2 | bytes 2621525 | solution.py:331
  144.9 5.3 %all-to-all-start = ((bf16[16,128,128]{2,1,0:T(8,128)(2,1)}), bf16[16,128,128]{2,1,0:T(8,128)(2,1)S(1)}, u32[]{:S(2)}, u32[]{:S(2)}) async-start(bf16[16,128,128]{2,1,0:T(8,128)(2,1)} %get-tuple-element.73), calls=%async_computation | async-start | bytes 1048576 | tf_op jit(solution)/shard_map/while/body/all_to_all | solution.py:331
  150.1 10.6 %all-to-all-done = bf16[16,128,128]{2,1,0:T(8,128)(2,1)S(1)} async-done(((bf16[16,128,128]{2,1,0:T(8,128)(2,1)}), bf16[16,128,128]{2,1,0:T(8,128)(2,1)S(1)}, u32[]{:S(2)}, u32[]{:S(2)}) %all-to-all-start) | async-done | bytes 524320 | tf_op jit(solution)/shard_map/while/body/all_to_all | solution.py:331
  160.7 0.8 copy.20
  161.5 2.4 %near.1 = (f32[128,512]{1,0:T(8,128)S(1)}, f32[128,128]{1,0:T(8,128)}) custom-call(s32[4]{0:T(128)S(1)} %compare_select_fusion.2.where_ref, bf16[2,128,512]{2,1,0:T(8,128)(2,1)S(1)} %bitcast.30, bf16[2048,512]{1,0:T(8,128)(2,1)S(1)} %bitcast.20, bf16[128,512]{1,0:T(8,128)(2,1)S(1)} %get-tuple-element.35.own_ref, ...), custom_call_target="tpu_custom_call" | custom-call | tf_op jit(solution)/shard_map/near/pallas_call | solution.py:332
  163.9 11.8 %collective-permute-done.2 = bf16[128,512]{1,0:T(8,128)(2,1)S(1)} collective-permute-done((bf16[128,512]{1,0:T(8,128)(2,1)S(1)}, bf16[128,512]{1,0:T(8,128)(2,1)S(1)}, u32[]{:S(2)}, u32[]{:S(2)}) %collective-permute-start.2) | collective-permute-done | bytes 131104 | tf_op jit(solution)/shard_map/ppermute | solution.py:37
  175.7 2.1 %all-gather.4 = bf16[256,512]{1,0:T(8,128)(2,1)S(1)} all-gather(bf16[128,512]{1,0:T(8,128)(2,1)S(1)} %collective-permute-done.2), channel_id=6, replica_groups={{0,1},{2,3},{4,5},{6,7},{8,9},{10,11},{12,13},{14,15},{16,17},{18,19},{..., dimensions={0}, use_global_device_ids=true | all-gather | bytes 393216 | tf_op jit(solution)/shard_map/all_gather | solution.py:26
  177.8 1.5 last.1
  (1 shorter events, 0.0 us)
Async XLA Ops:
  44.1 35.5 %copy-start = (bf16[1,2048,512]{2,1,0:T(8,128)(2,1)S(1)}, bf16[1,2048,512]{2,1,0:T(8,128)(2,1)}, u32[]{:S(2)}) copy-start(bf16[1,2048,512]{2,1,0:T(8,128)(2,1)} %param.22) | copy-start | bytes 6291460
  44.1 35.5 %copy-start.8 = (bf16[1,128,512]{2,1,0:T(8,128)(2,1)S(1)}, bf16[1,128,512]{2,1,0:T(8,128)(2,1)}, u32[]{:S(2)}) copy-start(bf16[1,128,512]{2,1,0:T(8,128)(2,1)} %param.15) | copy-start | bytes 393220
  79.6 52.9 %copy-start.1 = (bf16[1,2048,512]{2,1,0:T(8,128)(2,1)S(1)}, bf16[1,2048,512]{2,1,0:T(8,128)(2,1)}, u32[]{:S(2)}) copy-start(bf16[1,2048,512]{2,1,0:T(8,128)(2,1)} %param.19) | copy-start | bytes 6291460
  79.6 52.9 %copy-start.2 = (bf16[1,2048,128]{2,1,0:T(8,128)(2,1)S(1)}, bf16[1,2048,128]{2,1,0:T(8,128)(2,1)}, u32[]{:S(2)}) copy-start(bf16[1,2048,128]{2,1,0:T(8,128)(2,1)} %param.20) | copy-start | bytes 1572868
  79.6 52.9 %copy-start.3 = (bf16[1,2048,128]{2,1,0:T(8,128)(2,1)S(1)}, bf16[1,2048,128]{2,1,0:T(8,128)(2,1)}, u32[]{:S(2)}) copy-start(bf16[1,2048,128]{2,1,0:T(8,128)(2,1)} %param.21) | copy-start | bytes 1572868
  79.6 52.9 %copy-start.4 = (bf16[128,2048]{1,0:T(8,128)(2,1)S(1)}, bf16[128,2048]{1,0:T(8,128)(2,1)}, u32[]{:S(2)}) copy-start(bf16[128,2048]{1,0:T(8,128)(2,1)} %entering_ref.1) | copy-start | bytes 1572868
  79.6 52.9 %copy-start.5 = (bf16[1,2,128,128]{3,2,1,0:T(8,128)(2,1)S(1)}, bf16[1,2,128,128]{3,2,1,0:T(8,128)(2,1)}, u32[]{:S(2)}) copy-start(bf16[1,2,128,128]{3,2,1,0:T(8,128)(2,1)} %param.25) | copy-start | bytes 196612
  79.6 52.9 %copy-start.6 = (s32[17,128]{1,0:T(8,128)S(1)}, s32[17,128]{1,0:T(8,128)}, u32[]{:S(2)}) copy-start(s32[17,128]{1,0:T(8,128)} %segments_ref.1) | copy-start | bytes 26116
  79.6 52.9 %copy-start.7 = (f32[1,2048]{1,0:T(1,128)S(1)}, f32[1,2048]{1,0:T(1,128)}, u32[]{:S(2)}) copy-start(f32[1,2048]{1,0:T(1,128)} %gain_ref.1) | copy-start | bytes 24580
  80.1 55.3 %copy-start.9 = (bf16[128,512]{1,0:T(8,128)(2,1)}, bf16[128,512]{1,0:T(8,128)(2,1)S(1)}, u32[]{:S(2)}) copy-start(bf16[128,512]{1,0:T(8,128)(2,1)S(1)} %fusion) | copy-start | bytes 393220
  119.8 9.0 %collective-permute-start = (bf16[2,128,512]{2,1,0:T(8,128)(2,1)S(1)}, bf16[2,128,512]{2,1,0:T(8,128)(2,1)S(1)}, u32[]{:S(2)}, u32[]{:S(2)}) collective-permute-start(bf16[2,128,512]{2,1,0:T(8,128)(2,1)S(1)} %bitcast.34), channel_id=1, source_target_pairs={{0,64},{64,128},{128,192},{192,256},{256,320},{320,384},{384,448},... | collective-permute-start | bytes 786440 | tf_op jit(solution)/shard_map/ppermute | solution.py:42
  121.7 10.8 %collective-permute-start.1 = (bf16[128,128]{1,0:T(8,128)(2,1)S(1)}, bf16[128,128]{1,0:T(8,128)(2,1)S(1)}, u32[]{:S(2)}, u32[]{:S(2)}) collective-permute-start(bf16[128,128]{1,0:T(8,128)(2,1)S(1)} %get-tuple-element.32), channel_id=1, source_target_pairs={{0,64},{64,128},{128,192},{192,256},{256,320},{320,384},{384,448},... | collective-permute-start | bytes 98312 | tf_op jit(solution)/shard_map/ppermute | solution.py:42
  135.4 40.3 %collective-permute-start.2 = (bf16[128,512]{1,0:T(8,128)(2,1)S(1)}, bf16[128,512]{1,0:T(8,128)(2,1)S(1)}, u32[]{:S(2)}, u32[]{:S(2)}) collective-permute-start(bf16[128,512]{1,0:T(8,128)(2,1)S(1)} %get-tuple-element.34), channel_id=1, source_target_pairs={{0,2},{1,3},{2,0},{3,1},{4,6},{5,7},{6,4},{7,5},{8,10},{9,11},{10,... | collective-permute-start | bytes 393224 | tf_op jit(solution)/shard_map/ppermute | solution.py:37
  144.9 15.8 %all-to-all-start = ((bf16[16,128,128]{2,1,0:T(8,128)(2,1)}), bf16[16,128,128]{2,1,0:T(8,128)(2,1)S(1)}, u32[]{:S(2)}, u32[]{:S(2)}) async-start(bf16[16,128,128]{2,1,0:T(8,128)(2,1)} %get-tuple-element.73), calls=%async_computation | async-start | bytes 1048576 | tf_op jit(solution)/shard_map/while/body/all_to_all | solution.py:331
